TPU v7x, 32 devices: a whole 2x2x4 slice. The times are simulated.
32 devices in a mesh: grp: 4 (over y, x), seq: 8 (over z, core).
Axes of the slice: x: 2, y: 2, z: 4, core: 2. Of those that a mesh axis runs over, the one named last changes fastest.
Arguments:
- tokens: bfloat16 [20480, 1024], P(('grp', 'seq')), may hold values from -6 to 6
- cotangent: bfloat16 [20480, 1024], P(('grp', 'seq')), may hold values from -6 to 6
- query_key_value_weight: bfloat16 [3145728], P(('grp', 'seq')), may hold values from -0.1875 to 0.1875
- attention_out_weight: bfloat16 [1048576], P(('grp', 'seq')), may hold values from -1.5 to 1.5
- feedforward_in_weight: bfloat16 [4194304], P(('grp', 'seq')), may hold values from -0.1875 to 0.1875
- feedforward_out_weight: bfloat16 [4194304], P(('grp', 'seq')), may hold values from -0.09375 to 0.09375
- layer_norm_gains: float32 [2, 1024], replicated, may hold values from 0.25 to 1.75
- biases: float32 [10240], replicated, may hold values from -1.75 to 1.75
- adapter_down_matrices: bfloat16 [917504], P(('grp', 'seq')), may hold values from -0.1875 to 0.1875
- adapter_up_matrices: bfloat16 [1179648], P(('grp', 'seq')), may hold values from -0.75 to 0.75
- adapter_of_continuation: int32 [32, 1], P(('grp', 'seq')), may hold values from 0 to 7
Outputs:
- activations: bfloat16 [20480, 1024], P(('grp', 'seq'))
- input_grad: float32 [20480, 1024], P(('grp', 'seq'))
- down_grad: float32 [917504], P(('grp', 'seq'))
- up_grad: float32 [1179648], P(('grp', 'seq'))
Inputs may be any that keep to these rules, and one draw needn't show every extreme that they name: `adapter_of_continuation`: every one of the 8 adapters is named by some continuation.
All inputs are finite; a program needn't handle non-finite values.
Results may differ from a plain program's by a relative error of at most 0.012.
Values may be sent and summed in bfloat16 or wider, within the bound.
A program may use at most 256 MiB of HBM per device.

v0:
```python
import functools

import jax
import jax.numpy as jnp
from jax import lax
from jax.experimental import pallas as pl
from jax.experimental.pallas import tpu as pltpu
from jax.sharding import PartitionSpec as P

MODEL_WIDTH = 1024
HEADS = 16
HEAD_DIM = 64
HIDDEN_UNITS = 4096
ADAPTER_RANK = 16
ADAPTER_COUNT = 8
CONT_LEN = 512


EPSILON = 1e-05
NEGATIVE = -1e30


def product(left_side, right_side):
    return jnp.dot(left_side, right_side, preferred_element_type=jnp.float32)


def product_tn(left_side, right_side):
    return lax.dot_general(
        left_side, right_side, (((0,), (0,)), ((), ())), preferred_element_type=jnp.float32
    )


def product_nt(left_side, right_side):
    return lax.dot_general(
        left_side, right_side, (((1,), (1,)), ((), ())), preferred_element_type=jnp.float32
    )


def layer_norm(values, gain_vec, shift_vec):
    row_mean = jnp.mean(values, axis=-1, keepdims=True)
    centred = values - row_mean
    row_var = jnp.mean(centred * centred, axis=-1, keepdims=True)
    return centred * lax.rsqrt(row_var + EPSILON) * gain_vec + shift_vec


def unpack_sections(pieces, adapter_index):
    qkv_flat, out_flat, fc_flat, proj_flat, down_flat, up_flat = pieces
    every_down_matrix = down_flat.reshape(
        ADAPTER_COUNT, 3 * MODEL_WIDTH + HIDDEN_UNITS, ADAPTER_RANK
    )
    every_up_matrix = up_flat.reshape(ADAPTER_COUNT, ADAPTER_RANK, 5 * MODEL_WIDTH + HIDDEN_UNITS)
    down_rows = lax.dynamic_index_in_dim(every_down_matrix, adapter_index, 0, keepdims=False)
    up_cols = lax.dynamic_index_in_dim(every_up_matrix, adapter_index, 0, keepdims=False)
    weight_matrices = (
        qkv_flat.reshape(MODEL_WIDTH, 3 * MODEL_WIDTH),
        out_flat.reshape(MODEL_WIDTH, MODEL_WIDTH),
        fc_flat.reshape(MODEL_WIDTH, HIDDEN_UNITS),
        proj_flat.reshape(HIDDEN_UNITS, MODEL_WIDTH),
    )
    adapter_sections = (
        down_rows[:MODEL_WIDTH],
        down_rows[MODEL_WIDTH : 2 * MODEL_WIDTH],
        down_rows[2 * MODEL_WIDTH : 3 * MODEL_WIDTH],
        down_rows[3 * MODEL_WIDTH :],
        up_cols[:, : 3 * MODEL_WIDTH],
        up_cols[:, 3 * MODEL_WIDTH : 4 * MODEL_WIDTH],
        up_cols[:, 4 * MODEL_WIDTH : 4 * MODEL_WIDTH + HIDDEN_UNITS],
        up_cols[:, 4 * MODEL_WIDTH + HIDDEN_UNITS :],
    )
    return (weight_matrices, adapter_sections)


def visible(row_count, prompt_rows, prompt_total, key_count, seq_index):
    row_ids = jnp.arange(row_count, dtype=jnp.int32)[:, None]
    col_ids = jnp.arange(key_count, dtype=jnp.int32)[None, :]
    in_prompt = col_ids < prompt_total
    prompt_seen = in_prompt & (col_ids <= seq_index * prompt_rows + row_ids)
    later_seen = in_prompt | (col_ids - prompt_total <= row_ids - prompt_rows)
    return jnp.where(row_ids < prompt_rows, prompt_seen, later_seen)


def split_heads(values):
    return values.reshape(values.shape[0], HEADS, HEAD_DIM).transpose(1, 0, 2)


def merge_heads(values):
    return values.transpose(1, 0, 2).reshape(values.shape[1], HEADS * HEAD_DIM)


MESH = pl.DeviceIdType.MESH
SCALE2 = 0.125 * 1.4426950408889634
VMEM_LIMIT = 63 << 20


def gather_stages(groups, sizes, chunks, ins, outs, sems):
    grp_n, seq_n = groups
    z_n, y_n = seq_n // 2, grp_n // 2
    z_sem, x_sem, y_sem, d_sem, p_sem, s_sem, l_sem = sems
    g, s = lax.axis_index("grp"), lax.axis_index("seq")
    core, z = lax.rem(s, 2), s // 2
    gx, gy = lax.rem(g, 2), g // 2
    partner = (g, z * 2 + 1 - core)
    other_x = gy * 2 + 1 - gx
    x_next = (other_x, s)
    far_z = [lax.rem(z + d, z_n) for d in range(1, z_n)]
    far_y = [lax.rem(gy + d, y_n) for d in range(1, y_n)]
    y_next = [(y * 2 + gx, s) for y in far_y]

    def enter():
        peers = [partner, x_next] + y_next + [(g, far * 2 + core) for far in far_z]
        barrier = pltpu.get_barrier_semaphore()
        for peer in peers:
            pl.semaphore_signal(barrier, inc=1, device_id=peer, device_id_type=MESH)
        pl.semaphore_wait(barrier, len(peers))

    def place(ch, gg, ss):
        arr, row, rows, full = chunks[ch]
        block = gg * seq_n + ss if full else ss
        return outs[arr].at[pl.ds(pl.multiple_of(block * sizes[arr] + row, 16), rows)]

    def send(ch, src, gg, ss, sem, device):
        pltpu.make_async_remote_copy(
            src_ref=src,
            dst_ref=place(ch, gg, ss),
            send_sem=s_sem.at[ch],
            recv_sem=sem,
            device_id=device,
            device_id_type=MESH,
        ).start()

    def drain(ch, sem, count=1):
        arr, _, rows, _ = chunks[ch]
        block = outs[arr].at[pl.ds(0, count * rows)]
        pltpu.make_async_copy(block, block, sem).wait()

    def own(ch):
        arr, row, rows, full = chunks[ch]
        src = ins[arr].at[pl.ds(row, rows)]
        for far in far_z:
            send(ch, src, g, s, z_sem.at[ch, z], (g, far * 2 + core))
        if full:
            send(ch, src, g, s, x_sem.at[ch, z], x_next)
            for peer in y_next:
                send(ch, src, g, s, y_sem.at[ch, gy, z], peer)
        send(ch, src, g, s, p_sem.at[ch, 0], partner)
        pltpu.make_async_copy(src, place(ch, g, s), l_sem.at[ch]).start()

    def line(ch):
        for far in far_z:
            drain(ch, z_sem.at[ch, far])
            from_s = far * 2 + core
            src = place(ch, g, from_s)
            if chunks[ch][3]:
                send(ch, src, g, from_s, x_sem.at[ch, far], x_next)
                for peer in y_next:
                    send(ch, src, g, from_s, y_sem.at[ch, gy, far], peer)
            send(ch, src, g, from_s, p_sem.at[ch, 0], partner)

    def side(ch):
        if not chunks[ch][3]:
            return
        for far in range(z_n):
            from_s = far * 2 + core
            drain(ch, x_sem.at[ch, far])
            src = place(ch, other_x, from_s)
            if far % 2 == 0:
                for peer in y_next:
                    send(ch, src, other_x, from_s, d_sem.at[ch, gy, far], peer)
            send(ch, src, other_x, from_s, p_sem.at[ch, 1], partner)
            for y in far_y:
                drain(ch, y_sem.at[ch, y, far])
                from_g = y * 2 + gx
                src = place(ch, from_g, from_s)
                if far % 2 == 1:
                    send(ch, src, from_g, from_s, d_sem.at[ch, y, far], x_next)
                send(ch, src, from_g, from_s, p_sem.at[ch, 2], partner)

    def corner(ch):
        if not chunks[ch][3]:
            return
        for far in range(z_n):
            from_s = far * 2 + core
            for y in far_y:
                drain(ch, d_sem.at[ch, y, far])
                from_g = y * 2 + 1 - gx
                src = place(ch, from_g, from_s)
                send(ch, src, from_g, from_s, p_sem.at[ch, 3], partner)

    def ready(ch, kinds=range(4)):
        for kind in kinds if chunks[ch][3] else (0,):
            drain(ch, p_sem.at[ch, kind], z_n * (y_n - 1 if kind >= 2 else 1))
            if kind == 0:
                drain(ch, l_sem.at[ch])

    def finish(ch):
        sends = 2 * z_n - 1
        if chunks[ch][3]:
            sends += z_n * y_n
            sends += z_n * (y_n - 1)
            sends += z_n * (2 * y_n - 1)
        drain(ch, s_sem.at[ch], sends)

    steps = (own, line, side, corner)

    def tick(t):
        for lag, step in enumerate(steps):
            if 0 <= t - lag < len(chunks):
                step(t - lag)

    return enter, tick, ready, finish


def gather_plan(groups, shards, splits):
    grp_n, seq_n = groups
    chunks, shapes = [], []
    for i, (rows, cols, full) in enumerate(shards):
        part = rows // splits[i]
        chunks += [(i, j * part, part, full) for j in range(splits[i])]
        total = (grp_n if full else 1) * seq_n * rows
        shapes.append(jax.ShapeDtypeStruct((total, cols), jnp.bfloat16))
    dma, count = pltpu.SemaphoreType.DMA, len(chunks)
    sems = [
        dma((count, seq_n // 2)),
        dma((count, seq_n // 2)),
        dma((count, grp_n // 2, seq_n // 2)),
        dma((count, grp_n // 2, seq_n // 2)),
        dma((count, 4)),
        dma((count,)),
        dma((count,)),
    ]
    return [rows for rows, _, _ in shards], chunks, shapes, sems


def dot_nt(left, right):
    return lax.dot_general(
        left, right, (((1,), (1,)), ((), ())), preferred_element_type=jnp.float32
    )


def dot_nn(left, right):
    return lax.dot_general(
        left, right, (((1,), (0,)), ((), ())), preferred_element_type=jnp.float32
    )


def stacked_heads(pair):
    first = lax.broadcasted_iota(jnp.int32, pair.shape, 1) < HEAD_DIM
    zero = jnp.zeros_like(pair)
    return jnp.concatenate([jnp.where(first, pair, zero), jnp.where(first, zero, pair)], 0)


def row_groups(prompt_rows, prompt_total, later_rows):
    block = min(256, later_rows)
    return [(prompt_rows + i, block, prompt_total + i) for i in range(0, later_rows, block)]


def attention_forward(sizes, q_ref, k_ref, v_ref, ctx_ref, lse_ref, wide_ref):
    prompt_rows, prompt_total, later_rows = sizes
    seq = lax.axis_index("seq")
    wide_ref[:, :128] = v_ref[...]
    wide_ref[:, 128:] = jnp.ones((prompt_total + later_rows, 128), jnp.bfloat16)

    def finish(start, rows, row_max, summed):
        total = summed[:, 128:]
        mixed = summed[:, :128] / total
        log_total = row_max * SCALE2 + jnp.log2(total)
        first = lax.broadcasted_iota(jnp.int32, (rows, 128), 1) < HEAD_DIM
        ctx_ref[start : start + rows] = jnp.where(first, mixed[:rows], mixed[rows:]).astype(
            jnp.bfloat16
        )
        lse_ref[start : start + rows] = jnp.where(first, log_total[:rows], log_total[rows:])

    for start, rows, free in row_groups(prompt_rows, prompt_total, later_rows):
        queries = stacked_heads(q_ref[start : start + rows])
        open_scores = dot_nt(queries, k_ref[:free])
        edge_scores = dot_nt(queries, k_ref[free : free + rows])
        row = lax.broadcasted_iota(jnp.int32, (rows, rows), 0)
        key = lax.broadcasted_iota(jnp.int32, (rows, rows), 1)
        seen = key <= row
        edge_scores = jnp.where(jnp.concatenate([seen, seen], 0), edge_scores, NEGATIVE)
        row_max = jnp.maximum(
            jnp.max(open_scores, 1, keepdims=True), jnp.max(edge_scores, 1, keepdims=True)
        )
        scaled = row_max * SCALE2
        open_p = jnp.exp2(open_scores * SCALE2 - scaled).astype(jnp.bfloat16)
        edge_p = jnp.exp2(edge_scores * SCALE2 - scaled).astype(jnp.bfloat16)
        summed = dot_nn(open_p, wide_ref[:free]) + dot_nn(edge_p, wide_ref[free : free + rows])
        finish(start, rows, row_max, summed)
    scores = dot_nt(stacked_heads(q_ref[:prompt_rows]), k_ref[:prompt_total])
    row = lax.broadcasted_iota(jnp.int32, (prompt_rows, prompt_total), 0)
    key = lax.broadcasted_iota(jnp.int32, (prompt_rows, prompt_total), 1)
    seen = key <= row + seq * prompt_rows
    scores = jnp.where(jnp.concatenate([seen, seen], 0), scores, NEGATIVE)
    row_max = jnp.max(scores, 1, keepdims=True)
    p = jnp.exp2(scores * SCALE2 - row_max * SCALE2).astype(jnp.bfloat16)
    finish(0, prompt_rows, row_max, dot_nn(p, wide_ref[:prompt_total]))


def attention_backward(
    sizes, q_ref, k_ref, v_ref, d_ref, ctx_ref, lse_ref, dq_ref, k_sum, v_sum
):
    prompt_rows, prompt_total, later_rows = sizes
    seq = lax.axis_index("seq")
    keys_t = k_ref[...].astype(jnp.float32).T.astype(jnp.bfloat16)
    lse_t = lse_ref[...].T
    weighed_t = (d_ref[...].astype(jnp.float32) * ctx_ref[...].astype(jnp.float32)).T
    deltas = [
        jnp.sum(weighed_t[:HEAD_DIM], 0, keepdims=True),
        jnp.sum(weighed_t[HEAD_DIM:], 0, keepdims=True),
    ]
    totals = [lse_t[0:1], lse_t[HEAD_DIM : HEAD_DIM + 1]]

    def group(start, rows, count, mask):
        queries = stacked_heads(q_ref[start : start + rows])
        grads = stacked_heads(d_ref[start : start + rows])
        total = jnp.concatenate([t[:, start : start + rows] for t in totals], 1)
        delta = jnp.concatenate([t[:, start : start + rows] for t in deltas], 1)
        p = mask(jnp.exp2(dot_nt(k_ref[:count], queries) * SCALE2 - total))
        d_scores = (p * (dot_nt(v_ref[:count], grads) - delta)).astype(jnp.bfloat16)
        dq_t = dot_nn(keys_t[:, :count], d_scores)
        first = lax.broadcasted_iota(jnp.int32, (128, rows), 0) < HEAD_DIM
        dq = jnp.where(first, dq_t[:, :rows], dq_t[:, rows:]).T * 0.125
        dq_ref[start : start + rows] = dq.astype(jnp.bfloat16)
        return dot_nn(d_scores, queries), dot_nn(p.astype(jnp.bfloat16), grads)

    def causal(free, rows):
        def mask(p):
            key = lax.broadcasted_iota(jnp.int32, (rows, rows), 0)
            row = lax.broadcasted_iota(jnp.int32, (rows, rows), 1)
            seen = key <= row
            edge = jnp.where(jnp.concatenate([seen, seen], 1), p[free:], 0.0)
            return jnp.concatenate([p[:free], edge], 0)

        return mask

    def prompt_mask(p):
        key = lax.broadcasted_iota(jnp.int32, (prompt_total, prompt_rows), 0)
        row = lax.broadcasted_iota(jnp.int32, (prompt_total, prompt_rows), 1)
        seen = key <= row + seq * prompt_rows
        return jnp.where(jnp.concatenate([seen, seen], 1), p, 0.0)

    groups = row_groups(prompt_rows, prompt_total, later_rows)
    start, rows, free = groups[-1]
    k_sum[...], v_sum[...] = group(start, rows, free + rows, causal(free, rows))
    for start, rows, free in groups[:-1]:
        d_keys, d_values = group(start, rows, free + rows, causal(free, rows))
        k_sum[: free + rows] += d_keys
        v_sum[: free + rows] += d_values
    d_keys, d_values = group(0, prompt_rows, prompt_total, prompt_mask)
    k_sum[:prompt_total] += d_keys
    v_sum[:prompt_total] += d_values


UP_SECTIONS = (3 * MODEL_WIDTH, MODEL_WIDTH, HIDDEN_UNITS, MODEL_WIDTH)
UP_STARTS = (0, 768, 1024, 2048)
UP_FIRST = (0, 3 * MODEL_WIDTH, 4 * MODEL_WIDTH, 4 * MODEL_WIDTH + HIDDEN_UNITS)
QUARTER = (3 * MODEL_WIDTH + HIDDEN_UNITS) // 4
UP_QUARTER = sum(UP_SECTIONS) // 4
EARLY_COLS = QUARTER + UP_QUARTER - UP_STARTS[1]
TILE = 256


def for_blocks(count, body):
    def step(i, carry):
        body(pl.multiple_of(i * 128, 128))
        return carry

    lax.fori_loop(0, count // 128, step, 0)


def centre(values):
    centred = values - jnp.mean(values, axis=1, keepdims=True)
    var = jnp.mean(centred * centred, axis=1, keepdims=True)
    return centred, lax.rsqrt(var + EPSILON)


def normalize_rows(read, write, count, gain, shift):
    def body(start):
        centred, scale = centre(read(start))
        write(start, (centred * scale * gain + shift).astype(jnp.bfloat16))

    for_blocks(count, body)


def norm_pull(values, grads, gain):
    centred, scale = centre(values)
    unit = centred * scale
    grads = grads * gain
    along = jnp.mean(grads * unit, axis=1, keepdims=True)
    return scale * (grads - jnp.mean(grads, axis=1, keepdims=True) - unit * along)


def gelu_both(field):
    square = field * field
    bent = jnp.tanh(0.7978845608028654 * (field + 0.044715 * square * field))
    half = 0.5 * (1.0 + bent)
    slope = 0.7978845608028654 * (1.0 + 3.0 * 0.044715 * square)
    return field * half, half + 0.5 * field * (1.0 - bent * bent) * slope


def quarter_rows(rows, offset, part, across):
    rank = lax.broadcasted_iota(jnp.int32, (ADAPTER_RANK, rows), 0)
    row = lax.broadcasted_iota(jnp.int32, (ADAPTER_RANK, rows), 1)
    if across:
        rank = lax.broadcasted_iota(jnp.int32, (rows, ADAPTER_RANK), 1)
        row = lax.broadcasted_iota(jnp.int32, (rows, ADAPTER_RANK), 0)
    return (row == offset + (rank // 4) * 16 + (rank % 4) * 4 + part).astype(jnp.bfloat16)


def forward_and_gather(groups, ident, tokens, cotangent, gains, biases, shards, collective_id):
    rows = tokens.shape[0]
    prompt_rows = rows - CONT_LEN
    prompt_total = prompt_rows * groups[1]
    keys = prompt_total + CONT_LEN
    sizes = (prompt_rows, prompt_total, CONT_LEN)
    width, hidden_units = MODEL_WIDTH, HIDDEN_UNITS
    pairs = width // 128
    plan = [(prompt_rows, width, False)] + [(a.shape[0], a.shape[1], True) for a in shards]
    splits = [1, 1, 1, 2, 1, 2, 2]
    lengths, chunks, gathered, sems = gather_plan(groups, plan, splits)
    count = len(plan)
    dma = pltpu.SemaphoreType.DMA
    bf, f32 = jnp.bfloat16, jnp.float32

    def kernel(id_ref, tokens_ref, cot_ref, gains_ref, bias_ref, *refs):
        ins = (tokens_ref,) + refs[: count - 1]
        refs = refs[count - 1 :]
        q_out, kv_out, ctx_out, lse_out, act_out, dh_out, dc_out = refs[:7]
        early_out, inner_out, down_out, up_out = refs[7:11]
        outs, refs = refs[11 : 11 + count], refs[11 + count :]
        (
            prompt_v,
            norm_v,
            weight_v,
            w_out_v,
            q_v,
            kv_v,
            wide_v,
            ctx_v,
            lse_v,
            h_v,
            n_v,
            gl_v,
            gp_v,
            dn_v,
            downs_v,
            ups_v,
            down_v,
            up_v,
            low_v,
            turned_v,
            d_low,
            d_turned,
            acc_low,
            acc_turned,
            down_e,
            up_e,
            in_sem,
            out_sem,
        ) = refs[:28]
        enter, tick, ready, finish = gather_stages(groups, lengths, chunks, ins, outs, refs[28:])
        adapter = id_ref[0, 0]
        seq = lax.axis_index("seq")
        grp = lax.axis_index("grp")

        def load(src, dst, sem):
            copy = pltpu.make_async_copy(src, dst, in_sem.at[sem])
            copy.start()
            return copy

        stores, store_sem = [], iter(range(8))

        def store(src, dst):
            copy = pltpu.make_async_copy(src, dst, out_sem.at[next(store_sem)])
            copy.start()
            stores.append(copy)
            return copy

        def settle(copy):
            copy.wait()
            stores[:] = [other for other in stores if other is not copy]

        def bias(start, size):
            return bias_ref[:, pl.ds(pl.multiple_of(start, 128), size)]

        def tile(i, size=TILE, first=0):
            return pl.ds(pl.multiple_of(i * size + first, 128), size)

        def read_tokens(start):
            at = pl.multiple_of(start + prompt_rows, 128)
            return tokens_ref[pl.ds(at, 128)].astype(f32)

        def write_later(start, values):
            norm_v[pl.ds(pl.multiple_of(start + prompt_total, 128), 128)] = values

        def read_prompt(start):
            return prompt_v[pl.ds(start, 128)].astype(f32)

        def write_prompt(start, values):
            norm_v[pl.ds(start, 128)] = values

        def read_hidden(start):
            return h_v[pl.ds(start, 128)]

        def write_hidden(start, values):
            n_v[pl.ds(start, 128)] = values

        def inner(which, values, down):
            low_v[which] = dot_nt(values, down).astype(bf)
            turned_v[which] = dot_nt(down, values).astype(bf)

        def d_inner(which, values, up):
            d_low[which] = dot_nt(values, up).astype(bf)
            d_turned[which] = dot_nt(up, values).astype(bf)

        enter()
        tick(0)
        shift_one = bias_ref[:, :width]
        normalize_rows(read_tokens, write_later, CONT_LEN, gains_ref[0:1], shift_one)
        tick(1)
        ready(0)
        load(outs[0], prompt_v, 0).wait()
        normalize_rows(read_prompt, write_prompt, prompt_total, gains_ref[0:1], shift_one)
        tick(2)
        tick(3)
        tick(4)
        ready(1)
        copy_down = load(outs[1], downs_v, 1)
        tick(5)
        ready(2)
        copy_up = load(outs[2], ups_v, 2)
        copy_down.wait()
        copy_up.wait()
        at = lax.broadcasted_iota(jnp.int32, (ADAPTER_RANK, downs_v.shape[0]), 1)
        rank = lax.broadcasted_iota(jnp.int32, (ADAPTER_RANK, downs_v.shape[0]), 0)
        for part in range(4):
            chosen = (at == rank + (adapter * 64 + part * 16)).astype(bf)
            down_v[:, part * QUARTER : (part + 1) * QUARTER] = dot_nn(chosen, downs_v[...]).astype(
                bf
            )
            chosen = quarter_rows(ups_v.shape[0], adapter * 64, part, False)
            for first, start, size in zip(UP_FIRST, UP_STARTS, UP_SECTIONS):
                size //= 4
                up_v[:, first + part * size : first + (part + 1) * size] = dot_nn(
                    chosen, ups_v[:, start : start + size]
                ).astype(bf)
        down_out[...] = down_v[:, :width]
        up_out[...] = up_v[:, : 3 * width]
        inner(0, norm_v[prompt_total:], down_v[:, :width])
        inner_out[...] = turned_v[0]
        d_inner(3, cot_ref[prompt_rows:], up_v[:, UP_FIRST[3] :])
        tick(6)
        tick(7)
        ready(3)
        ready(4)
        load(outs[3], weight_v.at[:, : 3 * width], 3).wait()

        def later_tile(i):
            weight = weight_v[:, tile(i)]
            later = dot_nn(norm_v[prompt_total:], weight) + dot_nn(low_v[0], up_v[:, tile(i)])
            return weight, later

        def key_tile(i, carry):
            weight, later = later_tile(i)
            shift = jnp.where(i >= 8, bias(i * TILE + width, TILE), 0.0)
            to = tile(i - 4)
            kv_v[prompt_total:, to] = (later + shift).astype(bf)
            early = dot_nn(norm_v[:prompt_total], weight)
            kv_v[:prompt_total, to] = (early + shift).astype(bf)
            return carry

        def query_tile(i, carry):
            weight, later = later_tile(i)
            shift = bias(i * TILE + 2 * width, TILE)
            q_v[prompt_rows:, tile(i)] = (later + shift).astype(bf)
            mine = norm_v[pl.ds(pl.multiple_of(seq * prompt_rows, 128), prompt_rows)]
            q_v[:prompt_rows, tile(i)] = (dot_nn(mine, weight) + shift).astype(bf)
            return carry

        lax.fori_loop(4, 12, key_tile, 0)
        kv_store = store(kv_v, kv_out)
        tick(8)
        ready(5)
        load_out = load(outs[4], w_out_v, 4)
        lax.fori_loop(0, 4, query_tile, 0)
        q_store = store(q_v, q_out)

        def attend(i, carry):
            cols = pl.ds(pl.multiple_of(i * 128, 128), 128)
            values = pl.ds(pl.multiple_of(i * 128 + width, 128), 128)

            @pl.when(i == pairs // 2)
            def _():
                tick(9)

            attention_forward(
                sizes,
                q_v.at[:, cols],
                kv_v.at[:, cols],
                kv_v.at[:, values],
                ctx_v.at[:, cols],
                lse_v.at[:, cols],
                wide_v,
            )
            return carry

        lax.fori_loop(0, pairs, attend, 0)
        store(ctx_v, ctx_out)
        lse_store = store(lse_v, lse_out)
        tick(10)
        ready(6)
        ready(7)
        load_fc = load(outs[5], weight_v, 5)
        load_out.wait()
        inner(1, ctx_v[prompt_rows:], down_v[:, width : 2 * width])

        def out_tile(j, carry):
            cols = tile(j)
            mixed = dot_nn(ctx_v[...], w_out_v[:, cols]) + bias(j * TILE + 4 * width, TILE)
            mixed = tokens_ref[:, cols].astype(f32) + mixed
            extra = dot_nn(low_v[1], up_v[:, tile(j, first=UP_FIRST[1])])
            h_v[:prompt_rows, cols] = mixed[:prompt_rows]
            h_v[prompt_rows:, cols] = mixed[prompt_rows:] + extra
            return carry

        lax.fori_loop(0, 4, out_tile, 0)
        normalize_rows(
            read_hidden, write_hidden, rows, gains_ref[1:2], bias_ref[:, width : 2 * width]
        )
        inner(2, n_v[prompt_rows:], down_v[:, 2 * width : 3 * width])
        settle(lse_store)
        sum_v = lse_v

        def start_sums(start):
            at = pl.ds(start, 128)
            sum_v[at] = h_v[at] + bias_ref[:, 5 * width : 6 * width]
            dn_v[at] = jnp.zeros((128, width), f32)

        for_blocks(rows, start_sums)
        load_fc.wait()

        tiles = hidden_units // TILE

        def hidden_tile(i, carry):
            cols = tile(i)

            @pl.when(i == tiles // 2)
            def _():
                tick(11)

            wide = dot_nn(n_v[...], weight_v[:, cols]) + bias(i * TILE + 6 * width, TILE)
            extra = dot_nn(low_v[2], up_v[:, tile(i, first=UP_FIRST[2])])
            for at, field in (
                (slice(0, prompt_rows), wide[:prompt_rows]),
                (slice(prompt_rows, rows), wide[prompt_rows:] + extra),
            ):
                value, slope = gelu_both(field)
                gl_v[at, cols] = value.astype(bf)
                gp_v[at, cols] = slope.astype(bf)
            return carry

        lax.fori_loop(0, tiles, hidden_tile, 0)
        settle(kv_store)
        tick(12)

        df_v = norm_v.at[:rows]
        part_rows = hidden_units // 4
        for which in range(2):
            acc_low[which] = jnp.zeros((CONT_LEN, ADAPTER_RANK), f32)
            acc_turned[which] = jnp.zeros((ADAPTER_RANK, CONT_LEN), f32)
        gx, gy = lax.rem(grp, 2), grp // 2
        order = [grp, gy * 2 + 1 - gx, (1 - gy) * 2 + gx, (1 - gy) * 2 + 1 - gx]
        for kind, unit in enumerate(order):
            ready(8, (kind,))
            ready(9, (kind,))
            base = pl.multiple_of(unit * part_rows, part_rows)
            part = pl.ds(base, part_rows)
            down_part = pl.ds(pl.multiple_of(base + 3 * width, width), part_rows)
            up_part = pl.ds(pl.multiple_of(base + UP_FIRST[2], width), part_rows)
            slot = kv_v.at[:part_rows, (kind % 2) * width : (kind % 2 + 1) * width]
            load(outs[6].at[part], slot, 6 + kind % 2).wait()

            def d_hidden(j, carry, base=base, slot=slot):
                cols = tile(j, first=base)
                wide = dot_nt(cot_ref[...], slot[tile(j)])
                extra = dot_nn(d_low[3], down_v[:, tile(j, first=base + 3 * width)])
                slope = gp_v[:, cols].astype(f32)
                to = tile(j)
                df_v[:prompt_rows, to] = (wide[:prompt_rows] * slope[:prompt_rows]).astype(bf)
                later = (wide[prompt_rows:] + extra) * slope[prompt_rows:]
                df_v[prompt_rows:, to] = later.astype(bf)
                return carry

            lax.fori_loop(0, part_rows // TILE, d_hidden, 0)
            df_later = df_v[prompt_rows:]
            gl_later = gl_v[prompt_rows:, part]
            acc_low[0] += dot_nt(df_later, up_v[:, up_part])
            acc_turned[0] += dot_nt(up_v[:, up_part], df_later)
            acc_low[1] += dot_nt(gl_later, down_v[:, down_part])
            acc_turned[1] += dot_nt(down_v[:, down_part], gl_later)
            down_e[:, down_part] = dot_nn(d_turned[3], gl_later).astype(bf)
            up_e[:, up_part] = dot_nn(turned_v[2], df_later).astype(bf)

            def sums(j, carry, part=part, slot=slot):
                cols = tile(j)
                sum_v[:, cols] += dot_nn(gl_v[:, part], slot[:, cols])
                dn_v[:, cols] += dot_nt(df_v[...], weight_v[cols, part])
                return carry

            lax.fori_loop(0, width // TILE, sums, 0)

        d_low[2] = acc_low[0].astype(bf)
        d_turned[2] = acc_turned[0].astype(bf)
        low_v[3] = acc_low[1].astype(bf)
        turned_v[3] = acc_turned[1].astype(bf)
        act_v, attn_v, dc_v = prompt_v.at[:rows], q_v, norm_v.at[:rows]

        def last_tile(j, carry):
            cols = tile(j)
            dn_v[prompt_rows:, cols] += dot_nn(d_low[2], down_v[:, tile(j, first=2 * width)])
            act_v[:prompt_rows, cols] = sum_v[:prompt_rows, cols].astype(bf)
            extra = dot_nn(low_v[3], up_v[:, tile(j, first=UP_FIRST[3])])
            act_v[prompt_rows:, cols] = (sum_v[prompt_rows:, cols] + extra).astype(bf)
            return carry

        lax.fori_loop(0, width // TILE, last_tile, 0)
        store(act_v, act_out)
        settle(q_store)

        def pull_rows(start):
            at = pl.ds(start, 128)
            grads = cot_ref[at].astype(f32) + norm_pull(h_v[at], dn_v[at], gains_ref[1:2])
            dn_v[at] = grads
            attn_v[at] = grads.astype(bf)

        for_blocks(rows, pull_rows)
        store(dn_v, dh_out)
        d_inner(1, attn_v[prompt_rows:], up_v[:, UP_FIRST[1] : UP_FIRST[2]])

        def context_tile(j, carry):
            cols = tile(j)
            wide = dot_nt(attn_v[...], w_out_v[cols])
            extra = dot_nn(d_low[1], down_v[:, tile(j, first=width)])
            dc_v[:prompt_rows, cols] = wide[:prompt_rows].astype(bf)
            dc_v[prompt_rows:, cols] = (wide[prompt_rows:] + extra).astype(bf)
            return carry

        lax.fori_loop(0, width // TILE, context_tile, 0)
        store(dc_v, dc_out)
        down_e[:, :width] = jnp.zeros((ADAPTER_RANK, width), bf)
        down_e[:, width : 2 * width] = dot_nn(d_turned[1], ctx_v[prompt_rows:]).astype(bf)
        down_e[:, 2 * width : 3 * width] = dot_nn(d_turned[2], n_v[prompt_rows:]).astype(bf)
        up_e[:, UP_FIRST[1] : UP_FIRST[2]] = dot_nn(turned_v[1], attn_v[prompt_rows:]).astype(bf)
        up_e[:, UP_FIRST[3] :] = dot_nn(turned_v[3], cot_ref[prompt_rows:]).astype(bf)
        for quarter in range(4):
            early_out[quarter, :, :QUARTER] = down_e[:, quarter * QUARTER : (quarter + 1) * QUARTER]
        for section in range(1, 4):
            size = UP_SECTIONS[section] // 4
            moved = jnp.zeros((64, size), f32)
            for part in range(4):
                first = UP_FIRST[section] + part * size
                moved += dot_nn(quarter_rows(64, 0, part, True), up_e[:, first : first + size])
            first = QUARTER + UP_STARTS[section] - UP_STARTS[1]
            for quarter in range(4):
                early_out[quarter, :, first : first + size] = moved[
                    16 * quarter : 16 * quarter + 16
                ].astype(bf)
        for ch in range(len(chunks)):
            finish(ch)
        for copy in stores:
            copy.wait()

    vmem = pl.BlockSpec(memory_space=pltpu.VMEM)
    hbm = pl.BlockSpec(memory_space=pl.ANY)
    return pl.pallas_call(
        kernel,
        in_specs=[pl.BlockSpec(memory_space=pltpu.SMEM)] + [vmem] * (3 + count),
        out_specs=[hbm] * 7 + [vmem] * 4 + [hbm] * count,
        out_shape=[
            jax.ShapeDtypeStruct((rows, width), bf),
            jax.ShapeDtypeStruct((keys, 2 * width), bf),
            jax.ShapeDtypeStruct((rows, width), bf),
            jax.ShapeDtypeStruct((rows, width), f32),
            jax.ShapeDtypeStruct((rows, width), bf),
            jax.ShapeDtypeStruct((rows, width), f32),
            jax.ShapeDtypeStruct((rows, width), bf),
            jax.ShapeDtypeStruct((4, 16, EARLY_COLS), bf),
            jax.ShapeDtypeStruct((ADAPTER_RANK, CONT_LEN), bf),
            jax.ShapeDtypeStruct((ADAPTER_RANK, width), bf),
            jax.ShapeDtypeStruct((ADAPTER_RANK, 3 * width), bf),
        ]
        + gathered,
        scratch_shapes=[
            pltpu.VMEM((prompt_total, width), bf),
            pltpu.VMEM((keys, width), bf),
            pltpu.VMEM((width, hidden_units), bf),
            pltpu.VMEM((width, width), bf),
            pltpu.VMEM((rows, width), bf),
            pltpu.VMEM((keys, 2 * width), bf),
            pltpu.VMEM((keys, 256), bf),
            pltpu.VMEM((rows, width), bf),
            pltpu.VMEM((rows, width), f32),
            pltpu.VMEM((rows, width), f32),
            pltpu.VMEM((rows, width), bf),
            pltpu.VMEM((rows, hidden_units), bf),
            pltpu.VMEM((rows, hidden_units), bf),
            pltpu.VMEM((rows, width), f32),
            pltpu.VMEM(gathered[1].shape, bf),
            pltpu.VMEM(gathered[2].shape, bf),
            pltpu.VMEM((ADAPTER_RANK, 4 * QUARTER), bf),
            pltpu.VMEM((ADAPTER_RANK, 4 * UP_QUARTER), bf),
            pltpu.VMEM((4, CONT_LEN, ADAPTER_RANK), bf),
            pltpu.VMEM((4, ADAPTER_RANK, CONT_LEN), bf),
            pltpu.VMEM((4, CONT_LEN, ADAPTER_RANK), bf),
            pltpu.VMEM((4, ADAPTER_RANK, CONT_LEN), bf),
            pltpu.VMEM((2, CONT_LEN, ADAPTER_RANK), f32),
            pltpu.VMEM((2, ADAPTER_RANK, CONT_LEN), f32),
            pltpu.VMEM((ADAPTER_RANK, 4 * QUARTER), bf),
            pltpu.VMEM((ADAPTER_RANK, 4 * UP_QUARTER), bf),
            dma((8,)),
            dma((8,)),
        ]
        + sems,
        compiler_params=pltpu.CompilerParams(
            collective_id=collective_id, has_side_effects=True, vmem_limit_bytes=VMEM_LIMIT
        ),
    )(ident, tokens, cotangent, gains, biases, *shards)


def adapter_scratch(cols):
    dma = pltpu.SemaphoreType.DMA
    return [
        pltpu.VMEM((2, 16, cols), jnp.bfloat16),
        pltpu.VMEM((16, 128), jnp.bfloat16),
        pltpu.VMEM((3, 4, 16, cols), jnp.bfloat16),
        pltpu.VMEM((3, 4, 16, cols), jnp.bfloat16),
        pltpu.VMEM((4, 16, cols), jnp.float32),
        pltpu.VMEM((3, 16, cols), jnp.bfloat16),
        pltpu.VMEM((3, 16, cols), jnp.bfloat16),
        dma((3,)),
        dma((3,)),
        dma((3,)),
        dma((3,)),
        dma((3,)),
        dma((3,)),
    ]


def adapter_stages(term_ref, id_ref, out_ref, scratch):
    from_core, other_id, to_grp, from_grp, total, to_z, from_z = scratch[:7]
    a_send, a_recv, g_send, g_recv, z_send, z_recv = scratch[7:]
    g, s = lax.axis_index("grp"), lax.axis_index("seq")
    core, z = lax.rem(s, 2), s // 2
    other = 1 - core
    partner = (g, z * 2 + other)
    grps = [lax.rem(g + d, 4) for d in range(1, 4)]
    lines = [lax.rem(z + d, 4) for d in range(1, 4)]

    def enter():
        peers = [partner] + [(far, s) for far in grps] + [(g, far * 2 + core) for far in lines]
        barrier = pltpu.get_barrier_semaphore()
        for peer in peers:
            pl.semaphore_signal(barrier, inc=1, device_id=peer, device_id_type=MESH)
        pl.semaphore_wait(barrier, len(peers))

    def remote(src, dst, send_sem, recv_sem, device):
        return pltpu.make_async_remote_copy(
            src_ref=src,
            dst_ref=dst,
            send_sem=send_sem,
            recv_sem=recv_sem,
            device_id=device,
            device_id_type=MESH,
        )

    copies_a = [
        remote(term_ref.at[i * 2 + other], from_core.at[i], a_send.at[i], a_recv.at[i], partner)
        for i in range(2)
    ] + [remote(id_ref, other_id, a_send.at[2], a_recv.at[2], partner)]
    copies_g = [
        remote(to_grp.at[d], from_grp.at[d], g_send.at[d], g_recv.at[d], (grps[d], s))
        for d in range(3)
    ]
    copies_z = [
        remote(to_z.at[d], from_z.at[d], z_send.at[d], z_recv.at[d], (g, lines[d] * 2 + core))
        for d in range(3)
    ]

    def start(copies):
        for copy in copies:
            copy.start()

    def wait(copies):
        for copy in copies:
            copy.wait()

    def select():
        wait(copies_a)
        mine = id_ref[0:1, 0:1].astype(jnp.float32)
        theirs = other_id[0:1, 0:1].astype(jnp.float32)
        for d, grp in enumerate(grps + [g]):
            for slot in range(4):
                adapter = (grp * 2 + slot // 2).astype(jnp.float32)
                own_term = term_ref[(slot % 2) * 2 + core].astype(jnp.float32)
                other_term = from_core[slot % 2].astype(jnp.float32)
                picked = jnp.where(mine == adapter, own_term, 0.0) + jnp.where(
                    theirs == adapter, other_term, 0.0
                )
                if d < 3:
                    to_grp[d, slot] = picked.astype(jnp.bfloat16)
                else:
                    total[slot] = picked

    def add_grps():
        wait(copies_g)
        for slot in range(4):
            total[slot] += sum(from_grp[d, slot].astype(jnp.float32) for d in range(3))
        for d in range(3):
            to_z[d] = total[lines[d]].astype(jnp.bfloat16)

    def add_lines():
        wait(copies_z)
        out_ref[...] = total[z] + sum(from_z[d].astype(jnp.float32) for d in range(3))

    return (
        enter,
        lambda: start(copies_a),
        select,
        lambda: start(copies_g),
        add_grps,
        lambda: start(copies_z),
        add_lines,
    )


LATE_COLS = MODEL_WIDTH + UP_STARTS[1]


def backward_tail(
    groups, q, kv, d_ctx, ctx, lse, early, ident, tokens, d_hidden, gains, biases, w_qkv, adapters,
    collective_id,
):
    rows, keys, pairs = q.shape[0], kv.shape[0], q.shape[1] // 128
    prompt_rows, prompt_total = rows - CONT_LEN, keys - CONT_LEN
    sizes = (prompt_rows, prompt_total, CONT_LEN)
    width, z_n = MODEL_WIDTH, groups[1] // 2
    bf, f32 = jnp.bfloat16, jnp.float32
    dma = pltpu.SemaphoreType.DMA
    adapter_shapes = len(adapter_scratch(128))

    def kernel(
        q_ref, k_ref, v_ref, d_ref, ctx_ref, lse_ref, early_ref, id_ref, tokens_ref, gains_ref,
        bias_ref, inner_ref, down_ref, up_ref, dh_hbm, w_hbm, *refs
    ):
        x_out, down_out, up_out = refs[:3]
        k_sum, v_sum, dqkv_v, term_v, pair_in, to_line, from_line = refs[3:10]
        w_v, dh_v, dn_v, n_v, late_v, early_sum, late_sum = refs[10:17]
        p_send, p_recv, l_send, l_recv, in_sem, out_sem = refs[17:23]
        scratch = refs[23:]
        e_enter, e_core, e_select, e_grp, e_add, e_z, e_lines = adapter_stages(
            early_ref, id_ref, early_sum, scratch[:adapter_shapes]
        )
        _, l_core, l_select, l_grp, l_add, l_z, l_lines = adapter_stages(
            late_v, id_ref, late_sum, scratch[adapter_shapes:]
        )
        g, s = lax.axis_index("grp"), lax.axis_index("seq")
        core, z = lax.rem(s, 2), s // 2
        far_z = [lax.rem(z + d, z_n) for d in range(1, z_n)]
        step = pl.program_id(0)

        def across(i):
            return pltpu.make_async_remote_copy(
                src_ref=term_v.at[i, 1 - core],
                dst_ref=pair_in.at[i],
                send_sem=p_send.at[i],
                recv_sem=p_recv.at[i],
                device_id=(g, z * 2 + 1 - core),
                device_id_type=MESH,
            )

        def along(i, d):
            return pltpu.make_async_remote_copy(
                src_ref=to_line.at[i, d],
                dst_ref=from_line.at[i, d],
                send_sem=l_send.at[i, d],
                recv_sem=l_recv.at[i, d],
                device_id=(g, far_z[d] * 2 + core),
                device_id_type=MESH,
            )

        def pass_on(i):
            across(i).wait()
            for d, far in enumerate(far_z):
                both = term_v[i, core, far].astype(f32) + pair_in[i, far].astype(f32)
                to_line[i, d] = both.astype(bf)
                along(i, d).start()

        load_w = pltpu.make_async_copy(w_hbm, w_v, in_sem.at[0])
        load_dh = pltpu.make_async_copy(dh_hbm, dh_v, in_sem.at[1])

        @pl.when(step == 0)
        def _():
            e_enter()
            e_core()
            load_w.start()
            load_dh.start()

        cols = pl.ds(pl.multiple_of(step * 128, 128), 128)
        attention_backward(
            sizes, q_ref, k_ref, v_ref, d_ref, ctx_ref, lse_ref, dqkv_v.at[:, cols], k_sum, v_sum
        )
        for block in range(2 * z_n):
            at = slice(block * prompt_rows, (block + 1) * prompt_rows)
            half = block % 2, block // 2
            term_v[step, half[0], half[1], :, :128] = (k_sum[at] * 0.125).astype(bf)
            term_v[step, half[0], half[1], :, 128:] = v_sum[at].astype(bf)
        across(step).start()
        for part, (total, scale) in enumerate(((k_sum, 0.125), (v_sum, 1.0))):
            to = pl.ds(pl.multiple_of(step * 128 + (part + 1) * width, 128), 128)
            dqkv_v[prompt_rows:, to] = (total[prompt_total:] * scale).astype(bf)

        @pl.when(step >= 1)
        def _():
            pass_on(step - 1)

        @pl.when(step == 1)
        def _():
            e_select()
            e_grp()

            def read(start):
                return tokens_ref[pl.ds(pl.multiple_of(start + prompt_rows, 128), 128)].astype(f32)

            def write(start, values):
                n_v[pl.ds(start, 128)] = values

            normalize_rows(read, write, CONT_LEN, gains_ref[0:1], bias_ref[:, :width])

        @pl.when(step == pairs // 2)
        def _():
            e_add()
            e_z()

        @pl.when(step == pairs - 1)
        def _():
            later = dqkv_v[prompt_rows:]
            d_low = dot_nt(later, up_ref[...]).astype(bf)
            d_turned = dot_nt(up_ref[...], later).astype(bf)
            late_v[...] = jnp.zeros(late_v.shape, bf)
            late_v[0, :, :width] = dot_nn(d_turned, n_v[...]).astype(bf)
            size = UP_SECTIONS[0] // 4
            moved = jnp.zeros((64, size), f32)
            for part in range(4):
                grads = dot_nn(inner_ref[...], dqkv_v[prompt_rows:, part * size : (part + 1) * size])
                moved += dot_nn(quarter_rows(64, 0, part, True), grads.astype(bf))
            for quarter in range(4):
                late_v[quarter, :, width:] = moved[16 * quarter : 16 * quarter + 16].astype(bf)
            l_core()
            pass_on(pairs - 1)
            load_w.wait()
            load_dh.wait()

            def pull(first, count):
                def body(start):
                    at = pl.ds(pl.multiple_of(start + first, 128), 128)
                    values = tokens_ref[at].astype(f32)
                    dn_v[at] = dh_v[at] + norm_pull(values, dn_v[at], gains_ref[0:1])

                for_blocks(count, body)
                copy = pltpu.make_async_copy(
                    dn_v.at[first : first + count], x_out.at[first : first + count],
                    out_sem.at[0 if first else 1],
                )
                copy.start()
                return copy

            def later_tile(j, carry):
                to = pl.ds(pl.multiple_of(j * TILE, TILE), TILE)
                wide = dot_nt(dqkv_v[prompt_rows:], w_v[to]) + dot_nn(d_low, down_ref[:, to])
                dn_v[prompt_rows:, to] = wide
                return carry

            lax.fori_loop(0, width // TILE, later_tile, 0)
            l_select()
            l_grp()
            later_store = pull(prompt_rows, CONT_LEN)
            e_lines()

            def arrived(i, carry):
                total = term_v[i, core, z].astype(f32) + pair_in[i, z].astype(f32)
                for d in range(z_n - 1):
                    along(i, d).wait()
                    total = total + from_line[i, d].astype(f32)
                for part in range(2):
                    to = pl.ds(pl.multiple_of(i * 128 + (part + 1) * width, 128), 128)
                    dqkv_v[:prompt_rows, to] = total[:, part * 128 : part * 128 + 128].astype(bf)
                return carry

            lax.fori_loop(0, pairs, arrived, 0)
            l_add()
            l_z()

            def prompt_tile(j, carry):
                to = pl.ds(pl.multiple_of(j * TILE, TILE), TILE)
                dn_v[:prompt_rows, to] = dot_nt(dqkv_v[:prompt_rows], w_v[to])
                return carry

            lax.fori_loop(0, width // TILE, prompt_tile, 0)
            prompt_store = pull(0, prompt_rows)
            l_lines()
            down_out[:, :width] = early_sum[:, :width] + late_sum[:, :width]
            down_out[:, width:] = early_sum[:, width:QUARTER]
            up_out[:, : UP_STARTS[1]] = late_sum[:, width:]
            up_out[:, UP_STARTS[1] :] = early_sum[:, QUARTER:]
            later_store.wait()
            prompt_store.wait()

    def pair(i):
        return (0, i)

    row_spec = pl.BlockSpec((rows, 128), pair)
    key_spec = pl.BlockSpec((keys, 128), pair)
    whole = pl.BlockSpec(memory_space=pltpu.VMEM)
    hbm = pl.BlockSpec(memory_space=pl.ANY)
    return pl.pallas_call(
        kernel,
        grid=(pairs,),
        in_specs=[
            row_spec,
            key_spec,
            pl.BlockSpec((keys, 128), lambda i: (0, pairs + i)),
            row_spec,
            row_spec,
            row_spec,
        ]
        + [whole] * 8
        + [hbm] * 2,
        out_specs=[hbm, whole, whole],
        out_shape=[
            jax.ShapeDtypeStruct((rows, width), f32),
            jax.ShapeDtypeStruct((16, QUARTER), f32),
            jax.ShapeDtypeStruct((16, UP_QUARTER), f32),
        ],
        scratch_shapes=[
            pltpu.VMEM((keys, 128), f32),
            pltpu.VMEM((keys, 128), f32),
            pltpu.VMEM((rows, 3 * width), bf),
            pltpu.VMEM((pairs, 2, z_n, prompt_rows, 256), bf),
            pltpu.VMEM((pairs, z_n, prompt_rows, 256), bf),
            pltpu.VMEM((pairs, z_n - 1, prompt_rows, 256), bf),
            pltpu.VMEM((pairs, z_n - 1, prompt_rows, 256), bf),
            pltpu.VMEM((width, 3 * width), bf),
            pltpu.VMEM((rows, width), f32),
            pltpu.VMEM((rows, width), f32),
            pltpu.VMEM((CONT_LEN, width), bf),
            pltpu.VMEM((4, 16, LATE_COLS), bf),
            pltpu.VMEM((16, EARLY_COLS), f32),
            pltpu.VMEM((16, LATE_COLS), f32),
            dma((pairs,)),
            dma((pairs,)),
            dma((pairs, z_n - 1)),
            dma((pairs, z_n - 1)),
            dma((2,)),
            dma((2,)),
        ]
        + adapter_scratch(EARLY_COLS)
        + adapter_scratch(LATE_COLS),
        compiler_params=pltpu.CompilerParams(
            collective_id=collective_id, has_side_effects=True, vmem_limit_bytes=VMEM_LIMIT
        ),
    )(
        q, kv, kv, d_ctx, ctx, lse, early, ident, tokens, gains, biases, *adapters, d_hidden, w_qkv
    )


def local_general(
    tokens,
    cotangent,
    query_key_value_weight,
    attention_out_weight,
    feedforward_in_weight,
    feedforward_out_weight,
    layer_norm_gains,
    biases,
    adapter_down_matrices,
    adapter_up_matrices,
    adapter_of_continuation,
):
    row_count = tokens.shape[0]
    prompt_rows = row_count - CONT_LEN
    prompt_total = prompt_rows * lax.axis_size("seq")
    key_count = prompt_total + CONT_LEN
    seq_index = lax.axis_index("seq")
    adapter_index = adapter_of_continuation[0, 0]
    weight_shards = (
        query_key_value_weight,
        attention_out_weight,
        feedforward_in_weight,
        feedforward_out_weight,
        adapter_down_matrices,
        adapter_up_matrices,
    )
    gathered_rows = (
        lax.all_gather(weight_shards[0], ("grp", "seq"), axis=0, tiled=True),
        lax.all_gather(weight_shards[1], ("grp", "seq"), axis=0, tiled=True),
        lax.all_gather(weight_shards[2], ("grp", "seq"), axis=0, tiled=True),
        lax.all_gather(weight_shards[3], ("grp", "seq"), axis=0, tiled=True),
        lax.all_gather(weight_shards[4], ("grp", "seq"), axis=0, tiled=True),
        lax.all_gather(weight_shards[5], ("grp", "seq"), axis=0, tiled=True),
    )
    weight_matrices, adapter_sections = unpack_sections(gathered_rows, adapter_index)
    frozen_query_key_value, frozen_attention_out, frozen_feedforward_in, frozen_feedforward_out = (
        weight_matrices
    )
    (
        down_query_key_value,
        down_attention_out,
        down_feedforward_in,
        down_feedforward_out,
        up_query_key_value,
        up_attention_out,
        up_feedforward_in,
        up_feedforward_out,
    ) = adapter_sections
    shift_one = biases[:MODEL_WIDTH]
    shift_two = biases[MODEL_WIDTH : 2 * MODEL_WIDTH]
    query_key_value_bias = jnp.concatenate(
        [
            biases[2 * MODEL_WIDTH : 3 * MODEL_WIDTH],
            jnp.zeros((MODEL_WIDTH,), jnp.float32),
            biases[3 * MODEL_WIDTH : 4 * MODEL_WIDTH],
        ]
    )
    bias_out = biases[4 * MODEL_WIDTH : 5 * MODEL_WIDTH]
    bias_proj = biases[5 * MODEL_WIDTH : 6 * MODEL_WIDTH]
    bias_fc = biases[6 * MODEL_WIDTH :]
    inputs = tokens.astype(jnp.float32)
    normed_one = layer_norm(inputs, layer_norm_gains[0], shift_one).astype(jnp.bfloat16)
    inner_one = product(normed_one[prompt_rows:], down_query_key_value).astype(jnp.bfloat16)
    mixed_query_key_value = product(normed_one, frozen_query_key_value) + query_key_value_bias
    mixed_query_key_value = mixed_query_key_value.at[prompt_rows:].add(
        product(inner_one, up_query_key_value)
    )
    qkv_rows = mixed_query_key_value.astype(jnp.bfloat16)
    prompt_keys, prompt_values = (
        lax.all_gather(
            qkv_rows[:prompt_rows, MODEL_WIDTH : 2 * MODEL_WIDTH], "seq", axis=0, tiled=True
        ),
        lax.all_gather(qkv_rows[:prompt_rows, 2 * MODEL_WIDTH :], "seq", axis=0, tiled=True),
    )
    all_keys = jnp.concatenate(
        [prompt_keys, qkv_rows[prompt_rows:, MODEL_WIDTH : 2 * MODEL_WIDTH]], 0
    )
    all_values = jnp.concatenate([prompt_values, qkv_rows[prompt_rows:, 2 * MODEL_WIDTH :]], 0)
    allowed = visible(row_count, prompt_rows, prompt_total, key_count, seq_index)
    query_heads = split_heads(qkv_rows[:, :MODEL_WIDTH])
    key_heads = split_heads(all_keys)
    value_heads = split_heads(all_values)

    def forward_head(operands):
        query_head, key_head, value_head = operands
        scores = jnp.where(allowed, product_nt(query_head, key_head) * 0.125, NEGATIVE)
        row_max = jnp.max(scores, axis=1, keepdims=True)
        exp_scores = jnp.exp(scores - row_max)
        exp_total = jnp.sum(exp_scores, axis=1, keepdims=True)
        weights = (exp_scores / exp_total).astype(jnp.bfloat16)
        return (product(weights, value_head), (row_max + jnp.log(exp_total))[:, 0])

    head_contexts, log_total = lax.map(forward_head, (query_heads, key_heads, value_heads))
    attention_context = merge_heads(head_contexts).astype(jnp.bfloat16)
    inner_two = product(attention_context[prompt_rows:], down_attention_out).astype(jnp.bfloat16)
    attention_output = product(attention_context, frozen_attention_out) + bias_out
    attention_output = attention_output.at[prompt_rows:].add(product(inner_two, up_attention_out))
    hidden = inputs + attention_output
    normed_two = layer_norm(hidden, layer_norm_gains[1], shift_two).astype(jnp.bfloat16)
    inner_three = product(normed_two[prompt_rows:], down_feedforward_in).astype(jnp.bfloat16)
    before_activation = product(normed_two, frozen_feedforward_in) + bias_fc
    before_activation = before_activation.at[prompt_rows:].add(
        product(inner_three, up_feedforward_in)
    )
    activated_hidden = jax.nn.gelu(before_activation, approximate=True).astype(jnp.bfloat16)
    inner_four = product(activated_hidden[prompt_rows:], down_feedforward_out).astype(jnp.bfloat16)
    adapter_branch = product(activated_hidden, frozen_feedforward_out) + bias_proj
    adapter_branch = adapter_branch.at[prompt_rows:].add(product(inner_four, up_feedforward_out))
    outputs = (hidden + adapter_branch).astype(jnp.bfloat16)
    weight_matrices, adapter_sections = unpack_sections(
        (
            lax.all_gather(weight_shards[0], ("grp", "seq"), axis=0, tiled=True),
            lax.all_gather(weight_shards[1], ("grp", "seq"), axis=0, tiled=True),
            lax.all_gather(weight_shards[2], ("grp", "seq"), axis=0, tiled=True),
            lax.all_gather(weight_shards[3], ("grp", "seq"), axis=0, tiled=True),
            lax.all_gather(weight_shards[4], ("grp", "seq"), axis=0, tiled=True),
            lax.all_gather(weight_shards[5], ("grp", "seq"), axis=0, tiled=True),
        ),
        adapter_index,
    )
    frozen_query_key_value, frozen_attention_out, frozen_feedforward_in, frozen_feedforward_out = (
        weight_matrices
    )
    (
        down_query_key_value,
        down_attention_out,
        down_feedforward_in,
        down_feedforward_out,
        up_query_key_value,
        up_attention_out,
        up_feedforward_in,
        up_feedforward_out,
    ) = adapter_sections
    grad_inner_four = product_nt(cotangent[prompt_rows:], up_feedforward_out).astype(jnp.bfloat16)
    grad_act = product_nt(cotangent, frozen_feedforward_out)
    grad_act = grad_act.at[prompt_rows:].add(product_nt(grad_inner_four, down_feedforward_out))
    gelu_pull = jax.vjp(lambda field: jax.nn.gelu(field, approximate=True), before_activation)[1]
    grad_pre = gelu_pull(grad_act)[0].astype(jnp.bfloat16)
    grad_inner_three = product_nt(grad_pre[prompt_rows:], up_feedforward_in).astype(jnp.bfloat16)
    grad_normed_two = product_nt(grad_pre, frozen_feedforward_in)
    grad_normed_two = grad_normed_two.at[prompt_rows:].add(
        product_nt(grad_inner_three, down_feedforward_in)
    )
    second_pull = jax.vjp(lambda field: layer_norm(field, layer_norm_gains[1], shift_two), hidden)[
        1
    ]
    grad_hidden = cotangent.astype(jnp.float32) + second_pull(grad_normed_two)[0]
    grad_attn = grad_hidden.astype(jnp.bfloat16)
    grad_inner_two = product_nt(grad_attn[prompt_rows:], up_attention_out).astype(jnp.bfloat16)
    grad_context = product_nt(grad_attn, frozen_attention_out)
    grad_context = (
        grad_context.at[prompt_rows:]
        .add(product_nt(grad_inner_two, down_attention_out))
        .astype(jnp.bfloat16)
    )

    def backward_head(operands):
        query_head, key_head, value_head, grad_head, total_head = operands
        scores = jnp.where(allowed, product_nt(query_head, key_head) * 0.125, NEGATIVE)
        prob_full = jnp.exp(scores - total_head[:, None])
        weights = prob_full.astype(jnp.bfloat16)
        grad_weights = product_nt(grad_head, value_head)
        row_delta = jnp.sum(prob_full * grad_weights, axis=1, keepdims=True)
        grad_scores = (prob_full * (grad_weights - row_delta)).astype(jnp.bfloat16)
        return (
            product(grad_scores, key_head) * 0.125,
            product_tn(grad_scores, query_head) * 0.125,
            product_tn(weights, grad_head),
        )

    grad_q, grad_k, grad_v = lax.map(
        backward_head, (query_heads, key_heads, value_heads, split_heads(grad_context), log_total)
    )
    grad_query = merge_heads(grad_q)
    grad_keys = merge_heads(grad_k)
    grad_values = merge_heads(grad_v)
    own_keys, own_values = (
        lax.psum_scatter(
            grad_keys[:prompt_total].astype(jnp.bfloat16), "seq", scatter_dimension=0, tiled=True
        ).astype(jnp.float32),
        lax.psum_scatter(
            grad_values[:prompt_total].astype(jnp.bfloat16), "seq", scatter_dimension=0, tiled=True
        ).astype(jnp.float32),
    )
    grad_qkv = jnp.concatenate(
        [
            grad_query,
            jnp.concatenate([own_keys, grad_keys[prompt_total:]], 0),
            jnp.concatenate([own_values, grad_values[prompt_total:]], 0),
        ],
        1,
    ).astype(jnp.bfloat16)
    grad_inner_one = product_nt(grad_qkv[prompt_rows:], up_query_key_value).astype(jnp.bfloat16)
    grad_normed_one = product_nt(grad_qkv, frozen_query_key_value)
    grad_normed_one = grad_normed_one.at[prompt_rows:].add(
        product_nt(grad_inner_one, down_query_key_value)
    )
    first_pull = jax.vjp(lambda field: layer_norm(field, layer_norm_gains[0], shift_one), inputs)[1]
    input_grad = grad_hidden + first_pull(grad_normed_one)[0]
    down_term = jnp.concatenate(
        [
            product_tn(normed_one[prompt_rows:], grad_inner_one),
            product_tn(attention_context[prompt_rows:], grad_inner_two),
            product_tn(normed_two[prompt_rows:], grad_inner_three),
            product_tn(activated_hidden[prompt_rows:], grad_inner_four),
        ],
        0,
    )
    up_term = jnp.concatenate(
        [
            product_tn(inner_one, grad_qkv[prompt_rows:]),
            product_tn(inner_two, grad_attn[prompt_rows:]),
            product_tn(inner_three, grad_pre[prompt_rows:]),
            product_tn(inner_four, cotangent[prompt_rows:]),
        ],
        1,
    )
    select = (jnp.arange(ADAPTER_COUNT, dtype=jnp.int32) == adapter_index).astype(jnp.float32)
    down_grad, up_grad = (
        lax.psum_scatter(
            (select[:, None, None] * down_term[None]).reshape(-1),
            ("grp", "seq"),
            scatter_dimension=0,
            tiled=True,
        ),
        lax.psum_scatter(
            (select[:, None, None] * up_term[None]).reshape(-1),
            ("grp", "seq"),
            scatter_dimension=0,
            tiled=True,
        ),
    )
    return (outputs, input_grad, down_grad, up_grad)


def fast(
    tokens,
    cotangent,
    query_key_value_weight,
    attention_out_weight,
    feedforward_in_weight,
    feedforward_out_weight,
    layer_norm_gains,
    biases,
    adapter_down_matrices,
    adapter_up_matrices,
    adapter_of_continuation,
):
    groups = (lax.axis_size("grp"), lax.axis_size("seq"))
    up_cols = 5 * MODEL_WIDTH + HIDDEN_UNITS
    ups_shard = adapter_up_matrices.reshape(4, up_cols)
    up_parts, first = [], 0
    for size in UP_SECTIONS:
        up_parts.append(ups_shard[:, first : first + size].reshape(16, size // 4))
        first += size
    (
        queries,
        keys_values,
        context,
        log_total,
        outputs,
        grad_hidden,
        grad_context,
        early_term,
        inner_one,
        down_qkv,
        up_qkv,
        _,
        _,
        _,
        w_qkv,
        _,
        _,
        _,
    ) = forward_and_gather(
        groups,
        adapter_of_continuation,
        tokens,
        cotangent,
        layer_norm_gains,
        biases.reshape(1, -1),
        [
            adapter_down_matrices.reshape(-1, ADAPTER_RANK).T,
            jnp.concatenate(up_parts, 1),
            query_key_value_weight.reshape(-1, 3 * MODEL_WIDTH),
            attention_out_weight.reshape(-1, MODEL_WIDTH),
            feedforward_in_weight.reshape(-1, HIDDEN_UNITS),
            feedforward_out_weight.reshape(-1, MODEL_WIDTH),
        ],
        1,
    )
    ident = jnp.full((16, 128), adapter_of_continuation[0, 0], jnp.int32).astype(jnp.bfloat16)
    input_grad, down_grad, up_grad = backward_tail(
        groups,
        queries,
        keys_values,
        grad_context,
        context,
        log_total,
        early_term,
        ident,
        tokens,
        grad_hidden,
        layer_norm_gains,
        biases.reshape(1, -1),
        w_qkv,
        (inner_one, down_qkv, up_qkv),
        3,
    )
    down_grad = down_grad.T.reshape(-1)
    up_pieces = []
    for start, size in zip(UP_STARTS, UP_SECTIONS):
        up_pieces.append(up_grad[:, start : start + size // 4].reshape(4, -1))
    up_grad = jnp.concatenate(up_pieces, 1).reshape(-1)
    return (outputs, input_grad, down_grad, up_grad)


def solution(mesh):
    placed = (
        P(("grp", "seq"), None),
        P(("grp", "seq"), None),
        P(("grp", "seq")),
        P(("grp", "seq")),
        P(("grp", "seq")),
        P(("grp", "seq")),
        P(),
        P(),
        P(("grp", "seq")),
        P(("grp", "seq")),
        P(("grp", "seq"), None),
    )
    fits = mesh.shape["grp"] == 4 and mesh.shape["seq"] == 8
    return jax.shard_map(
        fast if fits else local_general,
        mesh=mesh,
        in_specs=placed,
        out_specs=(
            P(("grp", "seq"), None),
            P(("grp", "seq"), None),
            P(("grp", "seq")),
            P(("grp", "seq")),
        ),
        check_vma=False,
    )
```

profile of v0, /device:TPU:0, one launch (start us, length us, event | category | flops | bytes accessed | tf_op | source)
XLA Modules:
  0.0 308.4 jit_solution(14903879000955672497)
XLA Ops:
  0.6 0.0 copy-start.1
  0.6 0.0 copy-start.2
  0.7 0.0 copy-start.3
  0.7 1.0 reshape.63
  1.8 0.6 pad_maximum_fusion.refs_1_
  3.1 1.1 reshape.62
  4.2 0.8 copy.15
  5.0 1.8 reshape.70.refs_4_
  6.8 0.0 copy-done.1
  6.8 0.8 reshape.71.refs_5_
  7.6 0.0 copy-done.2
  7.6 0.8 reshape.68.refs_2_
  8.4 0.0 copy-done.3
  8.4 0.7 reshape.69.refs_3_
  9.0 206.2 %shard_map.138 = (bf16[640,1024]{1,0:T(8,128)(2,1)}, bf16[1536,2048]{1,0:T(8,128)(2,1)}, bf16[640,1024]{1,0:T(8,128)(2,1)}, f32[640,1024]{1,0:T(8,128)}, bf16[64...) custom-call(s32[1,1]{1,0:T(1,128)S(6)} %copy.20.id_ref, ...), custom_call_target="tpu_custom_call" | custom-call | tf_op jit(solution)/shard_map/pallas_call | solution.py:775
  215.3 0.6 broadcast_in_dim.3.id_ref
  215.9 83.1 %shard_map.139 = (f32[640,1024]{1,0:T(8,128)}, f32[16,1792]{1,0:T(8,128)}, f32[16,2304]{1,0:T(8,128)}) custom-call(bf16[640,1024]{1,0:T(8,128)(2,1)} %get-tuple-element.20.q_ref, bf16[1536,2048]{1,0:T(8,128)(2,1)} %get-tuple-element.21.k_ref.v_ref, bf16[1536,2048]{1,0:T(8,128)(2,1)} %get-tuple-element.21.k_ref.v_ref, ...), custom_call_target="tpu_custom_call" | custom-call | tf_op jit(solution)/shard_map/pallas_call | solution.py:1125
  299.0 0.8 slice.30
  299.9 0.8 slice.28
  300.7 0.7 fusion
  301.5 0.7 copy.17
  302.2 0.0 copy-start
  302.2 1.3 copy.16
  303.5 0.9 reshape.72
  304.5 2.5 copy.21
  306.9 0.0 copy-done
  306.9 1.5 copy.22
  (12 shorter events, 0.2 us)
Async XLA Ops:
  0.6 6.2 %copy-start.1 = (bf16[131072]{0:T(1024)(128)(2,1)S(1)}, bf16[131072]{0:T(1024)(128)(2,1)}, u32[]{:S(2)}) copy-start(bf16[131072]{0:T(1024)(128)(2,1)} %param.16) | copy-start | bytes 786436
  0.6 7.0 %copy-start.2 = (bf16[98304]{0:T(1024)(128)(2,1)S(1)}, bf16[98304]{0:T(1024)(128)(2,1)}, u32[]{:S(2)}) copy-start(bf16[98304]{0:T(1024)(128)(2,1)} %param.13) | copy-start | bytes 589828
  0.7 7.7 %copy-start.3 = (bf16[32768]{0:T(1024)(128)(2,1)S(1)}, bf16[32768]{0:T(1024)(128)(2,1)}, u32[]{:S(2)}) copy-start(bf16[32768]{0:T(1024)(128)(2,1)} %param.14) | copy-start | bytes 196612
  302.2 4.7 %copy-start = (f32[640,1024]{1,0:T(8,128)S(1)}, f32[640,1024]{1,0:T(8,128)}, u32[]{:S(2)}) copy-start(f32[640,1024]{1,0:T(8,128)} %get-tuple-element.43) | copy-start | bytes 7864324
where the time goes:
time: 309 us; the launch traced here: 308 us
  Pallas kernels  289 us (94%)
  local copies, waits for them, and re-layouts  17 us (6%)
    pallas_call x1, Pallas kernels, forward_and_gather(): pl.pallas_call(kernel, in_specs=[pl.BlockSpec(memory_space=pltpu.SMEM)] +...  206 us
    pallas_call x1, Pallas kernels, backward_tail(): pl.pallas_call(kernel, grid=(pairs,), in_specs=[row_spec, key_spec, pl.Bl...  83.1 us

commit v1 on v0

--- a/solution.py
+++ b/solution.py
@@ -114,9 +114,10 @@
         pl.semaphore_wait(barrier, len(peers))
 
     def place(ch, gg, ss):
-        arr, row, rows, full = chunks[ch]
+        arr, row, rows, col, cols, full = chunks[ch]
         block = gg * seq_n + ss if full else ss
-        return outs[arr].at[pl.ds(pl.multiple_of(block * sizes[arr] + row, 16), rows)]
+        at = pl.ds(pl.multiple_of(block * sizes[arr] + row, 16), rows)
+        return outs[arr].at[at, pl.ds(col, cols)]
 
     def send(ch, src, gg, ss, sem, device):
         pltpu.make_async_remote_copy(
@@ -129,56 +130,80 @@
         ).start()
 
     def drain(ch, sem, count=1):
-        arr, _, rows, _ = chunks[ch]
-        block = outs[arr].at[pl.ds(0, count * rows)]
+        arr, _, rows, col, cols, _ = chunks[ch]
+        block = outs[arr].at[pl.ds(0, count * rows), pl.ds(col, cols)]
         pltpu.make_async_copy(block, block, sem).wait()
 
+    def each(first, last, body):
+        def step(i, carry):
+            body(i)
+            return carry
+
+        lax.fori_loop(first, last, step, 0)
+
+    def shard(ch):
+        arr, row, rows, col, cols, _ = chunks[ch]
+        return ins[arr].at[pl.ds(row, rows), pl.ds(col, cols)]
+
     def own(ch):
-        arr, row, rows, full = chunks[ch]
-        src = ins[arr].at[pl.ds(row, rows)]
-        for far in far_z:
-            send(ch, src, g, s, z_sem.at[ch, z], (g, far * 2 + core))
-        if full:
-            send(ch, src, g, s, x_sem.at[ch, z], x_next)
-            for peer in y_next:
-                send(ch, src, g, s, y_sem.at[ch, gy, z], peer)
+        src = shard(ch)
+
+        def to_line(d):
+            send(ch, src, g, s, z_sem.at[ch, z], (g, lax.rem(z + d, z_n) * 2 + core))
+
+        each(1, z_n, to_line)
         send(ch, src, g, s, p_sem.at[ch, 0], partner)
         pltpu.make_async_copy(src, place(ch, g, s), l_sem.at[ch]).start()
 
+    def near(ch):
+        src = shard(ch)
+        send(ch, src, g, s, x_sem.at[ch, z], x_next)
+        for peer in y_next:
+            send(ch, src, g, s, y_sem.at[ch, gy, z], peer)
+
     def line(ch):
-        for far in far_z:
+        def relay(d):
+            far = lax.rem(z + d, z_n)
             drain(ch, z_sem.at[ch, far])
             from_s = far * 2 + core
             src = place(ch, g, from_s)
-            if chunks[ch][3]:
+            if chunks[ch][5]:
                 send(ch, src, g, from_s, x_sem.at[ch, far], x_next)
                 for peer in y_next:
                     send(ch, src, g, from_s, y_sem.at[ch, gy, far], peer)
             send(ch, src, g, from_s, p_sem.at[ch, 0], partner)
 
+        each(1, z_n, relay)
+
     def side(ch):
-        if not chunks[ch][3]:
+        if not chunks[ch][5]:
             return
-        for far in range(z_n):
-            from_s = far * 2 + core
-            drain(ch, x_sem.at[ch, far])
-            src = place(ch, other_x, from_s)
-            if far % 2 == 0:
-                for peer in y_next:
-                    send(ch, src, other_x, from_s, d_sem.at[ch, gy, far], peer)
-            send(ch, src, other_x, from_s, p_sem.at[ch, 1], partner)
-            for y in far_y:
-                drain(ch, y_sem.at[ch, y, far])
-                from_g = y * 2 + gx
-                src = place(ch, from_g, from_s)
-                if far % 2 == 1:
-                    send(ch, src, from_g, from_s, d_sem.at[ch, y, far], x_next)
-                send(ch, src, from_g, from_s, p_sem.at[ch, 2], partner)
+
+        def relay(half):
+            for odd in range(2):
+                far = half * 2 + odd
+                from_s = far * 2 + core
+                drain(ch, x_sem.at[ch, far])
+                src = place(ch, other_x, from_s)
+                if not odd:
+                    for peer in y_next:
+                        send(ch, src, other_x, from_s, d_sem.at[ch, gy, far], peer)
+                send(ch, src, other_x, from_s, p_sem.at[ch, 1], partner)
+                for y in far_y:
+                    drain(ch, y_sem.at[ch, y, far])
+                    from_g = y * 2 + gx
+                    src = place(ch, from_g, from_s)
+                    if odd:
+                        send(ch, src, from_g, from_s, d_sem.at[ch, y, far], x_next)
+                    send(ch, src, from_g, from_s, p_sem.at[ch, 2], partner)
+
+        each(0, z_n // 2, relay)
 
     def corner(ch):
-        if not chunks[ch][3]:
+        if not chunks[ch][5]:
             return
-        for far in range(z_n):
+
+        def relay(far):
             from_s = far * 2 + core
             for y in far_y:
                 drain(ch, d_sem.at[ch, y, far])
@@ -186,38 +211,43 @@
                 src = place(ch, from_g, from_s)
                 send(ch, src, from_g, from_s, p_sem.at[ch, 3], partner)
 
+        each(0, z_n, relay)
+
+    def ready_kind(ch, kind):
+        drain(ch, p_sem.at[ch, kind], z_n)
+        pl.when(kind == 0)(lambda: drain(ch, l_sem.at[ch]))
+
     def ready(ch, kinds=range(4)):
-        for kind in kinds if chunks[ch][3] else (0,):
+        for kind in kinds if chunks[ch][5] else (0,):
             drain(ch, p_sem.at[ch, kind], z_n * (y_n - 1 if kind >= 2 else 1))
             if kind == 0:
                 drain(ch, l_sem.at[ch])
 
     def finish(ch):
         sends = 2 * z_n - 1
-        if chunks[ch][3]:
+        if chunks[ch][5]:
             sends += z_n * y_n
             sends += z_n * (y_n - 1)
             sends += z_n * (2 * y_n - 1)
         drain(ch, s_sem.at[ch], sends)
 
-    steps = (own, line, side, corner)
+    steps = {"own": own, "near": near, "line": line, "side": side, "corner": corner}
 
     def tick(t):
-        for lag, step in enumerate(steps):
-            if 0 <= t - lag < len(chunks):
-                step(t - lag)
-
-    return enter, tick, ready, finish
-
-
-def gather_plan(groups, shards, splits):
+        for step, which in GATHER_ORDER[t]:
+            for ch in which:
+                steps[step](ch)
+
+    return enter, tick, ready, ready_kind, finish
+
+
+def gather_plan(groups, shards, chunks):
     grp_n, seq_n = groups
-    chunks, shapes = [], []
-    for i, (rows, cols, full) in enumerate(shards):
-        part = rows // splits[i]
-        chunks += [(i, j * part, part, full) for j in range(splits[i])]
+    shapes = []
+    for rows, cols, full in shards:
         total = (grp_n if full else 1) * seq_n * rows
         shapes.append(jax.ShapeDtypeStruct((total, cols), jnp.bfloat16))
+    chunks = [chunk + (shards[chunk[0]][2],) for chunk in chunks]
     dma, count = pltpu.SemaphoreType.DMA, len(chunks)
     sems = [
         dma((count, seq_n // 2)),
@@ -229,6 +259,35 @@
         dma((count,)),
     ]
     return [rows for rows, _, _ in shards], chunks, shapes, sems
+
+
+GATHER_ORDER = (
+    (("own", (0, 1, 2, 3)), ("near", (1, 2, 3, 4, 5, 6, 7, 8))),
+    (("own", (4, 5)), ("near", (9, 10, 11, 12, 13, 14)), ("line", (0,))),
+    (("own", (6,)), ("line", (1,))),
+    (("own", (7,)), ("line", (2,))),
+    (("side", (1,)), ("line", (3,))),
+    (("corner", (1,)), ("side", (2,)), ("line", (4,))),
+    (("corner", (2,)), ("side", (3,)), ("line", (5,))),
+    (("own", (8,)), ("corner", (3,)), ("side", (4,)), ("line", (6,))),
+    (("own", (9,)), ("corner", (4,)), ("side", (5,)), ("line", (7,))),
+    (("own", (10,)), ("corner", (5,)), ("side", (6,)), ("line", (8,))),
+    (("own", (11,)), ("corner", (6,)), ("side", (7,))),
+    (("line", (9,)),),
+    (("own", (12,)), ("corner", (7,)), ("side", (8,))),
+    (("line", (10,)),),
+    (("own", (13,)), ("corner", (8,)), ("side", (9,))),
+    (("line", (11,)),),
+    (("own", (14,)), ("corner", (9,)), ("side", (10,))),
+    (("line", (12,)),),
+    (("corner", (10,)), ("side", (11,))),
+    (("line", (13,)),),
+    (("corner", (11,)), ("side", (12,))),
+    (("line", (14,)),),
+    (("corner", (12,)), ("side", (13,))),
+    (("corner", (13,)), ("side", (14,))),
+    (("corner", (14,)),),
+)
 
 
 def dot_nt(left, right):
@@ -358,6 +417,7 @@
 UP_QUARTER = sum(UP_SECTIONS) // 4
 EARLY_COLS = QUARTER + UP_QUARTER - UP_STARTS[1]
 TILE = 256
+WIDE = 512
 
 
 def for_blocks(count, body):
@@ -416,9 +476,14 @@
     width, hidden_units = MODEL_WIDTH, HIDDEN_UNITS
     pairs = width // 128
     plan = [(prompt_rows, width, False)] + [(a.shape[0], a.shape[1], True) for a in shards]
-    splits = [1, 1, 1, 2, 1, 2, 2]
-    lengths, chunks, gathered, sems = gather_plan(groups, plan, splits)
     count = len(plan)
+    whole = [(i, 0, plan[i][0], 0, plan[i][1]) for i in range(count)]
+    part = plan[6][0] // 4
+    cut = [whole[0], (3, 0, plan[3][0], width, width), (3, 0, plan[3][0], 2 * width, width)]
+    cut += [whole[1], whole[2], (3, 0, plan[3][0], 0, width), whole[4]]
+    cut += [(5, 0, plan[5][0], i * width, width) for i in range(4)]
+    cut += [(6, i * part, part, 0, width) for i in range(4)]
+    lengths, chunks, gathered, sems = gather_plan(groups, plan, cut)
     dma = pltpu.SemaphoreType.DMA
     bf, f32 = jnp.bfloat16, jnp.float32
 
@@ -458,7 +523,7 @@
             in_sem,
             out_sem,
         ) = refs[:28]
-        enter, tick, ready, finish = gather_stages(groups, lengths, chunks, ins, outs, refs[28:])
+        enter, tick, ready, ready_kind, finish = gather_stages(groups, lengths, chunks, ins, outs, refs[28:])
         adapter = id_ref[0, 0]
         seq = lax.axis_index("seq")
         grp = lax.axis_index("grp")
@@ -521,14 +586,32 @@
         ready(0)
         load(outs[0], prompt_v, 0).wait()
         normalize_rows(read_prompt, write_prompt, prompt_total, gains_ref[0:1], shift_one)
-        tick(2)
-        tick(3)
-        tick(4)
+        for t in range(2, 6):
+            tick(t)
+
+        def weight_part(i, sem):
+            cols = slice(i * width, (i + 1) * width)
+            return load(outs[3].at[:, cols], weight_v.at[:, cols], sem)
+
+        def prompt_tile(i, carry):
+            shift = jnp.where(i >= 8, bias(i * TILE + width, TILE), 0.0)
+            early = dot_nn(norm_v[:prompt_total], weight_v[:, tile(i)])
+            kv_v[:prompt_total, tile(i - 4)] = (early + shift).astype(bf)
+            return carry
+
         ready(1)
-        copy_down = load(outs[1], downs_v, 1)
-        tick(5)
+        weight_part(1, 1).wait()
+        lax.fori_loop(4, 8, prompt_tile, 0)
+        tick(6)
         ready(2)
-        copy_up = load(outs[2], ups_v, 2)
+        weight_part(2, 2).wait()
+        lax.fori_loop(8, 12, prompt_tile, 0)
+        tick(7)
+        ready(3)
+        copy_down = load(outs[1], downs_v, 3)
+        tick(8)
+        ready(4)
+        copy_up = load(outs[2], ups_v, 4)
         copy_down.wait()
         copy_up.wait()
         at = lax.broadcasted_iota(jnp.int32, (ADAPTER_RANK, downs_v.shape[0]), 1)
@@ -549,39 +632,27 @@
         inner(0, norm_v[prompt_total:], down_v[:, :width])
         inner_out[...] = turned_v[0]
         d_inner(3, cot_ref[prompt_rows:], up_v[:, UP_FIRST[3] :])
-        tick(6)
-        tick(7)
-        ready(3)
-        ready(4)
-        load(outs[3], weight_v.at[:, : 3 * width], 3).wait()
-
         def later_tile(i):
             weight = weight_v[:, tile(i)]
-            later = dot_nn(norm_v[prompt_total:], weight) + dot_nn(low_v[0], up_v[:, tile(i)])
-            return weight, later
+            return dot_nn(norm_v[prompt_total:], weight) + dot_nn(low_v[0], up_v[:, tile(i)])
 
         def key_tile(i, carry):
-            weight, later = later_tile(i)
             shift = jnp.where(i >= 8, bias(i * TILE + width, TILE), 0.0)
-            to = tile(i - 4)
-            kv_v[prompt_total:, to] = (later + shift).astype(bf)
-            early = dot_nn(norm_v[:prompt_total], weight)
-            kv_v[:prompt_total, to] = (early + shift).astype(bf)
+            kv_v[prompt_total:, tile(i - 4)] = (later_tile(i) + shift).astype(bf)
             return carry
 
         def query_tile(i, carry):
-            weight, later = later_tile(i)
             shift = bias(i * TILE + 2 * width, TILE)
-            q_v[prompt_rows:, tile(i)] = (later + shift).astype(bf)
+            q_v[prompt_rows:, tile(i)] = (later_tile(i) + shift).astype(bf)
             mine = norm_v[pl.ds(pl.multiple_of(seq * prompt_rows, 128), prompt_rows)]
-            q_v[:prompt_rows, tile(i)] = (dot_nn(mine, weight) + shift).astype(bf)
+            q_v[:prompt_rows, tile(i)] = (dot_nn(mine, weight_v[:, tile(i)]) + shift).astype(bf)
             return carry
 
+        tick(9)
         lax.fori_loop(4, 12, key_tile, 0)
         kv_store = store(kv_v, kv_out)
-        tick(8)
         ready(5)
-        load_out = load(outs[4], w_out_v, 4)
+        weight_part(0, 5).wait()
         lax.fori_loop(0, 4, query_tile, 0)
         q_store = store(q_v, q_out)
 
@@ -589,9 +660,8 @@
             cols = pl.ds(pl.multiple_of(i * 128, 128), 128)
             values = pl.ds(pl.multiple_of(i * 128 + width, 128), 128)
 
-            @pl.when(i == pairs // 2)
-            def _():
-                tick(9)
+            for at in range(pairs):
+                pl.when(i == at)(functools.partial(tick, 10 + at))
 
             attention_forward(
                 sizes,
@@ -607,10 +677,16 @@
         lax.fori_loop(0, pairs, attend, 0)
         store(ctx_v, ctx_out)
         lse_store = store(lse_v, lse_out)
-        tick(10)
+        tick(18)
         ready(6)
+        load_out = load(outs[4], w_out_v, 6)
         ready(7)
-        load_fc = load(outs[5], weight_v, 5)
+
+        def hidden_part(i):
+            cols = slice(i * width, (i + 1) * width)
+            return load(outs[5].at[:, cols], weight_v.at[:, cols], 7 + i)
+
+        hidden_loads = [hidden_part(0)]
         load_out.wait()
         inner(1, ctx_v[prompt_rows:], down_v[:, width : 2 * width])
 
@@ -624,6 +700,7 @@
             return carry
 
         lax.fori_loop(0, 4, out_tile, 0)
+        tick(19)
         normalize_rows(
             read_hidden, write_hidden, rows, gains_ref[1:2], bias_ref[:, width : 2 * width]
         )
@@ -637,16 +714,10 @@
             dn_v[at] = jnp.zeros((128, width), f32)
 
         for_blocks(rows, start_sums)
-        load_fc.wait()
-
-        tiles = hidden_units // TILE
+        tick(20)
 
         def hidden_tile(i, carry):
             cols = tile(i)
-
-            @pl.when(i == tiles // 2)
-            def _():
-                tick(11)
 
             wide = dot_nn(n_v[...], weight_v[:, cols]) + bias(i * TILE + 6 * width, TILE)
             extra = dot_nn(low_v[2], up_v[:, tile(i, first=UP_FIRST[2])])
@@ -659,9 +730,16 @@
                 gp_v[at, cols] = slope.astype(bf)
             return carry
 
-        lax.fori_loop(0, tiles, hidden_tile, 0)
+        for i in range(4):
+            hidden_loads[i].wait()
+            if i < 3:
+                ready(8 + i)
+                hidden_loads.append(hidden_part(i + 1))
+            lax.fori_loop(i * 4, i * 4 + 4, hidden_tile, 0)
+            if i < 2:
+                tick(21 + i)
         settle(kv_store)
-        tick(12)
+        tick(23)
 
         df_v = norm_v.at[:rows]
         part_rows = hidden_units // 4
@@ -669,29 +747,32 @@
             acc_low[which] = jnp.zeros((CONT_LEN, ADAPTER_RANK), f32)
             acc_turned[which] = jnp.zeros((ADAPTER_RANK, CONT_LEN), f32)
         gx, gy = lax.rem(grp, 2), grp // 2
-        order = [grp, gy * 2 + 1 - gx, (1 - gy) * 2 + gx, (1 - gy) * 2 + 1 - gx]
-        for kind, unit in enumerate(order):
-            ready(8, (kind,))
-            ready(9, (kind,))
-            base = pl.multiple_of(unit * part_rows, part_rows)
+
+        def unit_part(kind, carry):
+            pl.when(kind == 1)(functools.partial(tick, 24))
+            for ch in range(11, 15):
+                ready_kind(ch, kind)
+            unit_x = lax.rem(gx + kind, 2)
+            unit_y = lax.rem(gy + kind // 2, 2)
+            base = pl.multiple_of((unit_y * 2 + unit_x) * part_rows, part_rows)
             part = pl.ds(base, part_rows)
             down_part = pl.ds(pl.multiple_of(base + 3 * width, width), part_rows)
             up_part = pl.ds(pl.multiple_of(base + UP_FIRST[2], width), part_rows)
-            slot = kv_v.at[:part_rows, (kind % 2) * width : (kind % 2 + 1) * width]
-            load(outs[6].at[part], slot, 6 + kind % 2).wait()
-
-            def d_hidden(j, carry, base=base, slot=slot):
-                cols = tile(j, first=base)
-                wide = dot_nt(cot_ref[...], slot[tile(j)])
-                extra = dot_nn(d_low[3], down_v[:, tile(j, first=base + 3 * width)])
+            slot = kv_v.at[:part_rows, :width]
+            load(outs[6].at[part], slot, 11).wait()
+
+            def d_hidden(j, carry):
+                cols = tile(j, WIDE, base)
+                wide = dot_nt(cot_ref[...], slot[tile(j, WIDE)])
+                extra = dot_nn(d_low[3], down_v[:, tile(j, WIDE, base + 3 * width)])
                 slope = gp_v[:, cols].astype(f32)
-                to = tile(j)
+                to = tile(j, WIDE)
                 df_v[:prompt_rows, to] = (wide[:prompt_rows] * slope[:prompt_rows]).astype(bf)
                 later = (wide[prompt_rows:] + extra) * slope[prompt_rows:]
                 df_v[prompt_rows:, to] = later.astype(bf)
                 return carry
 
-            lax.fori_loop(0, part_rows // TILE, d_hidden, 0)
+            lax.fori_loop(0, part_rows // WIDE, d_hidden, 0)
             df_later = df_v[prompt_rows:]
             gl_later = gl_v[prompt_rows:, part]
             acc_low[0] += dot_nt(df_later, up_v[:, up_part])
@@ -701,14 +782,16 @@
             down_e[:, down_part] = dot_nn(d_turned[3], gl_later).astype(bf)
             up_e[:, up_part] = dot_nn(turned_v[2], df_later).astype(bf)
 
-            def sums(j, carry, part=part, slot=slot):
-                cols = tile(j)
+            def sums(j, carry):
+                cols = tile(j, WIDE)
                 sum_v[:, cols] += dot_nn(gl_v[:, part], slot[:, cols])
                 dn_v[:, cols] += dot_nt(df_v[...], weight_v[cols, part])
                 return carry
 
-            lax.fori_loop(0, width // TILE, sums, 0)
-
+            lax.fori_loop(0, width // WIDE, sums, 0)
+            return carry
+
+        lax.fori_loop(0, 4, unit_part, 0)
         d_low[2] = acc_low[0].astype(bf)
         d_turned[2] = acc_turned[0].astype(bf)
         low_v[3] = acc_low[1].astype(bf)
@@ -817,7 +900,7 @@
             pltpu.VMEM((2, ADAPTER_RANK, CONT_LEN), f32),
             pltpu.VMEM((ADAPTER_RANK, 4 * QUARTER), bf),
             pltpu.VMEM((ADAPTER_RANK, 4 * UP_QUARTER), bf),
-            dma((8,)),
+            dma((13,)),
             dma((8,)),
         ]
         + sems,

time: 309 us -> 291 us (0.942)
  Pallas kernels: 289 us -> 271 us
    pallas_call x1, Pallas kernels: 206 us -> 190 us  [forward_and_gather(): pl.pallas_call(kernel, in_specs=[pl.BlockSpec(memory_space=pltpu.SMEM)] +...]
where the time goes in v1:
time: 291 us; the launch traced here: 290 us
  Pallas kernels  271 us (93%)
  local copies, waits for them, and re-layouts  17 us (6%)
    pallas_call x1, Pallas kernels, forward_and_gather(): pl.pallas_call(kernel, in_specs=[pl.BlockSpec(memory_space=pltpu.SMEM)] +...  190 us
    pallas_call x1, Pallas kernels, backward_tail(): pl.pallas_call(kernel, grid=(pairs,), in_specs=[row_spec, key_spec, pl.Bl...  80.7 us

profile of v1, /device:TPU:0, one launch (start us, length us, event | category | flops | bytes accessed | tf_op | source)
XLA Modules:
  0.0 290.1 jit_solution(6654871552900970760)
XLA Ops:
  0.6 0.0 copy-start.1
  0.6 0.0 copy-start.2
  0.7 0.0 copy-start.3
  0.7 1.0 reshape.63
  1.8 0.6 pad_maximum_fusion.refs_1_
  3.1 1.1 reshape.62
  4.2 0.8 copy.15
  5.0 1.8 reshape.70.refs_4_
  6.8 0.0 copy-done.1
  6.8 0.8 reshape.71.refs_5_
  7.6 0.0 copy-done.2
  7.6 0.8 reshape.68.refs_2_
  8.4 0.0 copy-done.3
  8.4 0.7 reshape.69.refs_3_
  9.0 190.2 %shard_map.138 = (bf16[640,1024]{1,0:T(8,128)(2,1)}, bf16[1536,2048]{1,0:T(8,128)(2,1)}, bf16[640,1024]{1,0:T(8,128)(2,1)}, f32[640,1024]{1,0:T(8,128)}, bf16[64...) custom-call(s32[1,1]{1,0:T(1,128)S(6)} %copy.20.id_ref, ...), custom_call_target="tpu_custom_call" | custom-call | tf_op jit(solution)/shard_map/pallas_call | solution.py:858
  199.3 0.6 broadcast_in_dim.3.id_ref
  199.9 80.7 %shard_map.139 = (f32[640,1024]{1,0:T(8,128)}, f32[16,1792]{1,0:T(8,128)}, f32[16,2304]{1,0:T(8,128)}) custom-call(bf16[640,1024]{1,0:T(8,128)(2,1)} %get-tuple-element.20.q_ref, bf16[1536,2048]{1,0:T(8,128)(2,1)} %get-tuple-element.21.k_ref.v_ref, bf16[1536,2048]{1,0:T(8,128)(2,1)} %get-tuple-element.21.k_ref.v_ref, ...), custom_call_target="tpu_custom_call" | custom-call | tf_op jit(solution)/shard_map/pallas_call | solution.py:1208
  280.6 0.8 slice.30
  281.5 0.8 slice.28
  282.4 0.7 fusion
  283.2 0.7 copy.17
  283.8 0.0 copy-start
  283.8 1.3 copy.16
  285.2 0.9 reshape.72
  286.1 2.5 copy.21
  288.6 0.0 copy-done
  288.6 1.5 copy.22
  (12 shorter events, 0.2 us)
Async XLA Ops:
  0.6 6.2 %copy-start.1 = (bf16[131072]{0:T(1024)(128)(2,1)S(1)}, bf16[131072]{0:T(1024)(128)(2,1)}, u32[]{:S(2)}) copy-start(bf16[131072]{0:T(1024)(128)(2,1)} %param.16) | copy-start | bytes 786436
  0.6 7.0 %copy-start.2 = (bf16[98304]{0:T(1024)(128)(2,1)S(1)}, bf16[98304]{0:T(1024)(128)(2,1)}, u32[]{:S(2)}) copy-start(bf16[98304]{0:T(1024)(128)(2,1)} %param.13) | copy-start | bytes 589828
  0.7 7.7 %copy-start.3 = (bf16[32768]{0:T(1024)(128)(2,1)S(1)}, bf16[32768]{0:T(1024)(128)(2,1)}, u32[]{:S(2)}) copy-start(bf16[32768]{0:T(1024)(128)(2,1)} %param.14) | copy-start | bytes 196612
  283.8 4.7 %copy-start = (f32[640,1024]{1,0:T(8,128)S(1)}, f32[640,1024]{1,0:T(8,128)}, u32[]{:S(2)}) copy-start(f32[640,1024]{1,0:T(8,128)} %get-tuple-element.43) | copy-start | bytes 7864324

commit v2 on v1

--- a/solution.py
+++ b/solution.py
@@ -1140,6 +1140,8 @@
                 late_v[quarter, :, width:] = moved[16 * quarter : 16 * quarter + 16].astype(bf)
             l_core()
             pass_on(pairs - 1)
+            l_select()
+            l_grp()
             load_w.wait()
             load_dh.wait()
 
@@ -1164,9 +1166,9 @@
                 return carry
 
             lax.fori_loop(0, width // TILE, later_tile, 0)
-            l_select()
-            l_grp()
             later_store = pull(prompt_rows, CONT_LEN)
+            l_add()
+            l_z()
             e_lines()
 
             def arrived(i, carry):
@@ -1180,8 +1182,6 @@
                 return carry
 
             lax.fori_loop(0, pairs, arrived, 0)
-            l_add()
-            l_z()
 
             def prompt_tile(j, carry):
                 to = pl.ds(pl.multiple_of(j * TILE, TILE), TILE)

time: 291 us -> 290 us (level)
  no operation moved by 1% of the time
where the time goes in v2:
time: 290 us
  Pallas kernels  271 us (93%)
  local copies, waits for them, and re-layouts  17 us (6%)
    pallas_call x1, Pallas kernels, forward_and_gather(): pl.pallas_call(kernel, in_specs=[pl.BlockSpec(memory_space=pltpu.SMEM)] +...  190 us
    pallas_call x1, Pallas kernels, backward_tail(): pl.pallas_call(kernel, grid=(pairs,), in_specs=[row_spec, key_spec, pl.Bl...  80.3 us

profile of v2, /device:TPU:0, one launch (start us, length us, event | category | flops | bytes accessed | tf_op | source)
XLA Modules:
  0.0 289.7 jit_solution(4488992694036468676)
XLA Ops:
  0.6 0.0 copy-start.1
  0.6 0.0 copy-start.2
  0.7 0.0 copy-start.3
  0.7 1.0 reshape.63
  1.8 0.6 pad_maximum_fusion.refs_1_
  3.1 1.1 reshape.62
  4.2 0.8 copy.15
  5.0 1.8 reshape.70.refs_4_
  6.8 0.0 copy-done.1
  6.8 0.8 reshape.71.refs_5_
  7.6 0.0 copy-done.2
  7.6 0.8 reshape.68.refs_2_
  8.4 0.0 copy-done.3
  8.4 0.7 reshape.69.refs_3_
  9.0 190.2 %shard_map.138 = (bf16[640,1024]{1,0:T(8,128)(2,1)}, bf16[1536,2048]{1,0:T(8,128)(2,1)}, bf16[640,1024]{1,0:T(8,128)(2,1)}, f32[640,1024]{1,0:T(8,128)}, bf16[64...) custom-call(s32[1,1]{1,0:T(1,128)S(6)} %copy.20.id_ref, ...), custom_call_target="tpu_custom_call" | custom-call | tf_op jit(solution)/shard_map/pallas_call | solution.py:858
  199.3 0.6 broadcast_in_dim.3.id_ref
  199.9 80.3 %shard_map.139 = (f32[640,1024]{1,0:T(8,128)}, f32[16,1792]{1,0:T(8,128)}, f32[16,2304]{1,0:T(8,128)}) custom-call(bf16[640,1024]{1,0:T(8,128)(2,1)} %get-tuple-element.20.q_ref, bf16[1536,2048]{1,0:T(8,128)(2,1)} %get-tuple-element.21.k_ref.v_ref, bf16[1536,2048]{1,0:T(8,128)(2,1)} %get-tuple-element.21.k_ref.v_ref, ...), custom_call_target="tpu_custom_call" | custom-call | tf_op jit(solution)/shard_map/pallas_call | solution.py:1208
  280.2 0.8 slice.30
  281.1 0.8 slice.28
  282.0 0.7 fusion
  282.8 0.7 copy.17
  283.4 0.0 copy-start
  283.4 1.3 copy.16
  284.8 0.9 reshape.72
  285.7 2.5 copy.21
  288.2 0.0 copy-done
  288.2 1.5 copy.22
  (12 shorter events, 0.2 us)
Async XLA Ops:
  0.6 6.2 %copy-start.1 = (bf16[131072]{0:T(1024)(128)(2,1)S(1)}, bf16[131072]{0:T(1024)(128)(2,1)}, u32[]{:S(2)}) copy-start(bf16[131072]{0:T(1024)(128)(2,1)} %param.16) | copy-start | bytes 786436
  0.6 7.0 %copy-start.2 = (bf16[98304]{0:T(1024)(128)(2,1)S(1)}, bf16[98304]{0:T(1024)(128)(2,1)}, u32[]{:S(2)}) copy-start(bf16[98304]{0:T(1024)(128)(2,1)} %param.13) | copy-start | bytes 589828
  0.7 7.7 %copy-start.3 = (bf16[32768]{0:T(1024)(128)(2,1)S(1)}, bf16[32768]{0:T(1024)(128)(2,1)}, u32[]{:S(2)}) copy-start(bf16[32768]{0:T(1024)(128)(2,1)} %param.14) | copy-start | bytes 196612
  283.4 4.7 %copy-start = (f32[640,1024]{1,0:T(8,128)S(1)}, f32[640,1024]{1,0:T(8,128)}, u32[]{:S(2)}) copy-start(f32[640,1024]{1,0:T(8,128)} %get-tuple-element.43) | copy-start | bytes 7864324
